TPU v7x, 512 devices: a whole 4x4x16 slice. The times are simulated.
512 devices in a mesh: gx: 32 (over y_lo, z), gy: 16 (over x, y_hi, core).
Axes of the slice: x: 4, y: 4 (y_hi: 2, y_lo: 2; y = y_hi * 2 + y_lo), z: 16, core: 2. Of those that a mesh axis runs over, the one named last changes fastest.
Arguments:
- mass_per_volume: float32 [256, 512, 128], P('gx', 'gy'), may hold values from 0.5 to 2
- momentum: float32 [3, 256, 512, 128], P(None, 'gx', 'gy'), may hold values from -0.9 to 0.9
- energy: float32 [256, 512, 128], P('gx', 'gy'), may hold values from 3 to 8
Outputs:
- tendency: float32 [5, 256, 512, 128], P(None, 'gx', 'gy')
- advanced: float32 [5, 256, 512, 128], P(None, 'gx', 'gy')
All inputs are finite; a program needn't handle non-finite values.
Results may differ from a plain program's by a relative error of at most 0.00016.
Values sent between devices are 32-bit elements; how exact they have to be, the bound alone decides.
A program may use at most 64 MiB of HBM per device.

v0:
```python
import jax
import jax.numpy as jnp
import numpy as np
from jax import lax
from jax.sharding import PartitionSpec as P

CX = 8
CY = 8
NZ = 512
HALO = 4


heat_ratio = 1.4
shear_resistance_reference = 0.08
sutherland_power_law = 0.7
prandtl = 0.72
section_step = 0.05
compact_alpha = 1.0 / 3.0
compact_near = 14.0 / 9.0
compact_far = 1.0 / 9.0


def padded(array, sides, width):
    for axis, dim in sides:
        devices, length = (lax.axis_size(axis), array.shape[dim])
        up = [(i, (i + 1) % devices) for i in range(devices)]
        down = [(j, i) for i, j in up]
        last = lax.slice_in_dim(array, length - width, length, axis=dim)
        initial = lax.slice_in_dim(array, 0, width, axis=dim)
        before = lax.ppermute(last, axis, up)
        after = lax.ppermute(initial, axis, down)
        array = jnp.concatenate([before, array, after], axis=dim)
    return array


def tridiagonal_inverse_product(length, stencil):
    solved = np.array(stencil)
    upper_ratio = np.zeros(length)
    for row_index in range(length):
        if row_index == 0:
            pivot_value = 1.0
            solved[row_index] = solved[row_index] / pivot_value
        else:
            pivot_value = 1.0 - compact_alpha * upper_ratio[row_index - 1]
            solved[row_index] = (
                solved[row_index] - compact_alpha * solved[row_index - 1]
            ) / pivot_value
        upper_ratio[row_index] = compact_alpha / pivot_value
    for row_index in range(length - 2, -1, -1):
        solved[row_index] = solved[row_index] - upper_ratio[row_index] * solved[row_index + 1]
    return solved


def compact_matrix(block_size, margin):
    length = block_size + 2 * margin
    stencil = compact_near / 2.0 * (np.eye(length, k=1) - np.eye(length, k=-1))
    stencil = stencil + compact_far / 4.0 * (np.eye(length, k=2) - np.eye(length, k=-2))
    inverse_product = tridiagonal_inverse_product(length, stencil)
    return inverse_product[margin : margin + block_size].astype(np.float32)


def pitch_matrix(total, block_size):
    matrix = compact_matrix(block_size, HALO)
    result = np.zeros((total, total), np.float32)
    rows_all = np.arange(total)
    block_start = rows_all // block_size * block_size
    for offset in range(block_size + 2 * HALO):
        columns = (block_start - HALO + offset) % total
        result[rows_all, columns] += matrix[rows_all % block_size, offset]
    return result


def span_matrix(total):
    offsets = np.arange(total)[:, None] - np.arange(total)[None, :]
    angles = np.pi * offsets / total
    signs = np.where(offsets % 2 == 0, 1.0, -1.0)
    sines = np.where(offsets == 0, 1.0, np.sin(angles))
    result = np.where(offsets == 0, 0.0, np.pi / total * signs * np.cos(angles) / sines)
    return result.astype(np.float32)


def right_side(conserved, gradients_of, derive_x, derive_y, derive_z):
    mass_per_volume = conserved[0]
    momentum = conserved[1:4]
    energy = conserved[4]
    local_speed_vector = momentum / mass_per_volume
    kinetic = 0.5 * jnp.sum(momentum * local_speed_vector, axis=0)
    normal_force_per_area = (heat_ratio - 1.0) * (energy - kinetic)
    thermal_state = normal_force_per_area / mass_per_volume
    basic_quantities = jnp.concatenate([local_speed_vector, thermal_state[None]], 0)
    gradients = gradients_of(basic_quantities)
    shear_resistance = shear_resistance_reference * jnp.power(thermal_state, sutherland_power_law)
    conductivity = shear_resistance * heat_ratio / ((heat_ratio - 1.0) * prandtl)
    dilatation = gradients[0][0] + gradients[1][1] + gradients[2][2]
    derivers = (derive_x, derive_y, derive_z)
    accumulated = None
    for direction in range(3):
        stress_column = [
            shear_resistance * (gradients[direction][component] + gradients[component][direction])
            for component in range(3)
        ]
        stress_column[direction] = (
            stress_column[direction] - 2.0 / 3.0 * shear_resistance * dilatation
        )
        fluxes = [momentum[direction]]
        for component in range(3):
            moment_flux = (
                momentum[component] * local_speed_vector[direction] - stress_column[component]
            )
            if component == direction:
                moment_flux = moment_flux + normal_force_per_area
            fluxes.append(moment_flux)
        work_term = (
            stress_column[0] * local_speed_vector[0]
            + stress_column[1] * local_speed_vector[1]
            + stress_column[2] * local_speed_vector[2]
        )
        fluxes.append(
            (energy + normal_force_per_area) * local_speed_vector[direction]
            - work_term
            - conductivity * gradients[direction][3]
        )
        divergence_part = derivers[direction](jnp.stack(fluxes))
        accumulated = divergence_part if accumulated is None else accumulated + divergence_part
    return -accumulated


def per_device(mass_per_volume, momentum, energy):
    conserved = jnp.concatenate([mass_per_volume[None], momentum, energy[None]], 0)
    highest = lax.Precision.HIGHEST
    x_matrix = jnp.asarray(compact_matrix(CX, HALO))
    z_matrix = jnp.asarray(span_matrix(NZ))

    def apply_x(extended):
        return jnp.einsum("il,flab->fiab", x_matrix, extended, precision=highest)

    def flux_x(values):
        return apply_x(padded(values, (("gx", 1),), HALO))

    y_matrix = jnp.asarray(pitch_matrix(conserved.shape[3], CY))

    def apply_y(values):
        return jnp.einsum("fabk,jk->fabj", values, y_matrix, precision=highest)

    def derive_span(values):
        lines = jnp.transpose(
            lax.all_to_all(values, "gy", split_axis=3, concat_axis=2, tiled=True), (0, 1, 3, 2)
        )
        derived = jnp.einsum("fack,jk->facj", lines, z_matrix, precision=highest)
        returned = lax.all_to_all(derived, "gy", split_axis=3, concat_axis=2, tiled=True)
        return jnp.transpose(returned, (0, 1, 3, 2))

    def gradients_of(basic_quantities):
        extended = padded(basic_quantities, (("gx", 1),), HALO)
        return (apply_x(extended), apply_y(basic_quantities), derive_span(basic_quantities))

    tendency = right_side(conserved, gradients_of, flux_x, apply_y, derive_span)
    advanced = conserved + section_step * tendency
    return (tendency, advanced)


def solution(mesh):
    in_specs = (P("gx", "gy", None), P(None, "gx", "gy", None), P("gx", "gy", None))
    out_specs = (P(None, "gx", "gy", None), P(None, "gx", "gy", None))
    return jax.shard_map(
        per_device, mesh=mesh, in_specs=in_specs, out_specs=out_specs, check_vma=False
    )
```

profile of v0, /device:TPU:1, one launch (start us, length us, event | category | flops | bytes accessed | tf_op | source)
XLA Modules:
  0.0 195.7 jit_solution(11590446967682339407)
XLA Ops:
  1.6 1.3 broadcast_divide_fusion
  2.9 1.9 copy_divide_fusion
  5.6 2.9 %copy.103 = f32[4,8,32,128]{2,1,0,3:T(8,128)S(1)} copy(f32[4,8,32,128]{3,1,2,0:T(8,128)} %pad_maximum_fusion) | data formatting | bytes 1048576 | tf_op jit(solution)/shard_map/concatenate | solution.py:90
  8.5 1.7 reshape.16
  10.2 10.2 %all-to-all-start = ((f32[16,1,8192]{2,1,0:T(1,128)}), f32[16,1,8192]{2,1,0:T(1,128)S(1)}, u32[]{:S(2)}, u32[]{:S(2)}) async-start(f32[16,1,8192]{2,1,0:T(1,128)} %reshape.16), calls=%async_computation | async-start | bytes 1048576 | tf_op jit(solution)/shard_map/all_to_all | solution.py:147
  21.2 1.9 collective-permute-start
  23.2 9.5 %collective-permute-start.1 = (f32[4,4,32,128]{3,1,2,0:T(4,128)S(1)}, f32[4,4,32,128]{3,1,2,0:T(4,128)}, u32[]{:S(2)}, u32[]{:S(2)}) collective-permute-start(f32[4,4,32,128]{3,1,2,0:T(4,128)S(1)} %get-tuple-element.27), channel_id=1, source_target_pairs={{16,0},{32,16},{48,32},{64,48},{80,64},{96,80},{112,96},{128,112},... | collective-permute-start | bytes 786440 | tf_op jit(solution)/shard_map/ppermute | solution.py:31
  33.2 2.8 %reduce = f32[16,8192]{1,0:T(8,128)} reduce(f32[16,1,8192]{2,1,0:T(1,128)S(1)} %all-to-all-done, f32[]{:T(128)} %broadcast.6), dimensions={1}, to_apply=%all_to_all.52.reduce_sub_computation | reduce | bytes 1048580 | tf_op jit(solution)/shard_map/all_to_all | solution.py:147
  36.0 1.7 reshape.17
  37.7 2.6 %copy.105 = f32[4,8,16,32,8]{3,2,4,1,0:T(8,128)} copy(f32[4,8,16,32,8]{3,1,0,4,2:T(8,128)S(1)} %bitcast.281) | data formatting | bytes 1048576 | tf_op jit(solution)/shard_map/all_to_all | solution.py:147
  40.3 2.4 %all_to_all.55 = f32[4,8,512,8]{2,3,1,0:T(8,128)S(1)} reshape(f32[4,8,16,32,8]{3,2,4,1,0:T(8,128)} %copy.105) | data formatting | bytes 1048576 | tf_op jit(solution)/shard_map/all_to_all | solution.py:147
  42.7 1.1 fusion.27
  43.8 7.4 %copy.106 = f32[4,8,8,512]{2,1,0,3:T(8,128)} copy(f32[4,8,8,512]{3,2,1,0:T(8,128)S(1)} %fusion.27) | data formatting | bytes 1048576 | tf_op jit(solution)/shard_map/fack,jk->facj/dot_general | solution.py:149
  51.2 7.3 %reshape.18 = f32[16,1,8192]{2,1,0:T(1,128)} reshape(f32[512,4,8,8]{3,2,1,0:T(8,128)} %bitcast.271) | data formatting | bytes 1048576
  58.5 8.2 %all-to-all-start.1 = ((f32[16,1,8192]{2,1,0:T(1,128)}), f32[16,1,8192]{2,1,0:T(1,128)S(1)}, u32[]{:S(2)}, u32[]{:S(2)}) async-start(f32[16,1,8192]{2,1,0:T(1,128)} %reshape.18), calls=%async_computation.1 | async-start | bytes 1048576 | tf_op jit(solution)/shard_map/all_to_all | solution.py:150
  67.4 1.4 fusion.66
  68.8 2.7 %convolution_bitcast_fusion = f32[4,8,32,128]{3,1,2,0:T(8,128)} fusion(f32[8,16,1,1]{1,0,3,2:T(8,128)S(1)} %copy-done.23, f32[4,4,32,128]{3,1,2,0:T(4,128)} %collective-permute-done.1, f32[1,8,32,128]{3,1,2,0:T(8,128)S(1)} %bitcast.275, f32[3,8,32,128]{3,1,2,0:T(8,128)S(1)} %get-tuple-element.28, f32[4,4,32,128]{3,1,2,0:T(4,128)} %collective-permute-done), kind=kOutput, calls=%fused_computation.10 | convolution fusion | flops 25952256 | bytes 1573376 | tf_op jit(solution)/shard_map/il,flab->fiab/dot_general | solution.py:135
  71.5 6.3 %all-to-all-done.1 = f32[16,1,8192]{2,1,0:T(1,128)S(1)} async-done(((f32[16,1,8192]{2,1,0:T(1,128)}), f32[16,1,8192]{2,1,0:T(1,128)S(1)}, u32[]{:S(2)}, u32[]{:S(2)}) %all-to-all-start.1) | async-done | bytes 524320 | tf_op jit(solution)/shard_map/all_to_all | solution.py:150
  77.9 1.9 reduce.1
  79.8 6.7 %reshape.19 = f32[512,4,8,8]{3,2,1,0:T(8,128)} reshape(f32[16,8192]{1,0:T(8,128)S(1)} %reduce.1) | data formatting | bytes 1048576
  86.4 5.2 %copy.107 = f32[4,8,8,16,32]{4,2,3,1,0:T(8,128)S(1)} copy(f32[4,8,8,16,32]{2,1,0,4,3:T(8,128)} %bitcast.270) | data formatting | bytes 1048576 | tf_op jit(solution)/shard_map/all_to_all | solution.py:150
  91.6 1.4 copy.108
  93.0 1.8 bitcast_dynamic-update-slice_fusion.2
  94.8 1.7 bitcast_dynamic-update-slice_fusion.1
  96.5 1.9 bitcast_dynamic-update-slice_fusion
  98.5 1.0 bitcast_dynamic-update-slice_fusion.7
  102.1 2.2 %copy.117 = f32[5,8,32,128]{2,1,0,3:T(8,128)S(1)} copy(f32[5,8,32,128]{3,1,2,0:T(8,128)} %get-tuple-element.20) | data formatting | bytes 1310720 | tf_op jit(solution)/shard_map/stack | solution.py:123
  104.3 2.0 %reshape.20 = f32[16,1,10240]{2,1,0:T(1,128)} reshape(f32[128,5,8,32]{3,2,1,0:T(8,128)S(1)} %bitcast.276) | data formatting | bytes 1310720
  106.3 4.8 %all-to-all-start.2 = ((f32[16,1,10240]{2,1,0:T(1,128)}), f32[16,1,10240]{2,1,0:T(1,128)S(1)}, u32[]{:S(2)}, u32[]{:S(2)}) async-start(f32[16,1,10240]{2,1,0:T(1,128)} %reshape.20), calls=%async_computation.2 | async-start | bytes 1310720 | tf_op jit(solution)/shard_map/all_to_all | solution.py:147
  111.1 1.8 bitcast_dynamic-update-slice_fusion.4
  113.9 9.7 %all-to-all-done.2 = f32[16,1,10240]{2,1,0:T(1,128)S(1)} async-done(((f32[16,1,10240]{2,1,0:T(1,128)}), f32[16,1,10240]{2,1,0:T(1,128)S(1)}, u32[]{:S(2)}, u32[]{:S(2)}) %all-to-all-start.2) | async-done | bytes 655392 | tf_op jit(solution)/shard_map/all_to_all | solution.py:147
  123.6 3.2 %reduce.2 = f32[16,10240]{1,0:T(8,128)} reduce(f32[16,1,10240]{2,1,0:T(1,128)S(1)} %all-to-all-done.2, f32[]{:T(128)} %broadcast.6), dimensions={1}, to_apply=%all_to_all.60.reduce_sub_computation | reduce | bytes 1310724 | tf_op jit(solution)/shard_map/all_to_all | solution.py:147
  126.7 1.9 reshape.21
  128.7 3.0 %copy.119 = f32[5,8,16,32,8]{3,2,4,1,0:T(8,128)} copy(f32[5,8,16,32,8]{3,1,0,4,2:T(8,128)S(1)} %bitcast.277) | data formatting | bytes 1310720 | tf_op jit(solution)/shard_map/all_to_all | solution.py:147
  131.7 2.6 %all_to_all.63 = f32[5,8,512,8]{2,3,1,0:T(8,128)S(1)} reshape(f32[5,8,16,32,8]{3,2,4,1,0:T(8,128)} %copy.119) | data formatting | bytes 1310720 | tf_op jit(solution)/shard_map/all_to_all | solution.py:147
  134.3 1.2 fusion.25
  135.5 5.5 %copy.120 = f32[5,8,8,512]{2,1,0,3:T(8,128)} copy(f32[5,8,8,512]{3,2,1,0:T(8,128)S(1)} %fusion.25) | data formatting | bytes 1310720 | tf_op jit(solution)/shard_map/fack,jk->facj/dot_general | solution.py:149
  141.0 9.1 %reshape.22 = f32[16,1,10240]{2,1,0:T(1,128)} reshape(f32[512,5,8,8]{3,2,1,0:T(8,128)} %bitcast.268) | data formatting | bytes 1310720
  150.2 5.0 %all-to-all-start.3 = ((f32[16,1,10240]{2,1,0:T(1,128)}), f32[16,1,10240]{2,1,0:T(1,128)S(1)}, u32[]{:S(2)}, u32[]{:S(2)}) async-start(f32[16,1,10240]{2,1,0:T(1,128)} %reshape.22), calls=%async_computation.3 | async-start | bytes 1310720 | tf_op jit(solution)/shard_map/all_to_all | solution.py:150
  155.2 1.9 collective-permute-start.2
  157.2 5.7 %collective-permute-start.3 = (f32[5,4,32,128]{3,1,2,0:T(4,128)}, f32[5,4,32,128]{3,1,2,0:T(4,128)}, u32[]{:S(2)}, u32[]{:S(2)}) collective-permute-start(f32[5,4,32,128]{3,1,2,0:T(4,128)} %get-tuple-element.25), channel_id=1, source_target_pairs={{16,0},{32,16},{48,32},{64,48},{80,64},{96,80},{112,96},{128,112},... | collective-permute-start | bytes 983048 | tf_op jit(solution)/shard_map/ppermute | solution.py:31
  163.1 1.5 fusion.71
  164.7 5.3 %all-to-all-done.3 = f32[16,1,10240]{2,1,0:T(1,128)S(1)} async-done(((f32[16,1,10240]{2,1,0:T(1,128)}), f32[16,1,10240]{2,1,0:T(1,128)S(1)}, u32[]{:S(2)}, u32[]{:S(2)}) %all-to-all-start.3) | async-done | bytes 655392 | tf_op jit(solution)/shard_map/all_to_all | solution.py:150
  170.0 2.2 %reduce.3 = f32[16,10240]{1,0:T(8,128)S(1)} reduce(f32[16,1,10240]{2,1,0:T(1,128)S(1)} %all-to-all-done.3, f32[]{:T(128)} %broadcast.6), dimensions={1}, to_apply=%all_to_all.64.reduce_sub_computation | reduce | bytes 1310724 | tf_op jit(solution)/shard_map/all_to_all | solution.py:150
  172.1 10.4 %reshape.23 = f32[512,5,8,8]{3,2,1,0:T(8,128)} reshape(f32[16,10240]{1,0:T(8,128)S(1)} %reduce.3) | data formatting | bytes 1310720
  182.6 6.6 %copy.121 = f32[5,8,8,16,32]{4,2,3,1,0:T(8,128)S(1)} copy(f32[5,8,8,16,32]{2,1,0,4,3:T(8,128)} %bitcast.269) | data formatting | bytes 1310720 | tf_op jit(solution)/shard_map/all_to_all | solution.py:150
  189.2 1.8 copy.122
  191.1 2.8 %maximum_add_fusion = (f32[5,8,32,128]{3,1,2,0:T(8,128)S(1)}, f32[5,8,32,128]{3,1,2,0:T(8,128)S(1)}) fusion(f32[1,8,32,128]{3,1,2,0:T(8,128)S(1)} %copy-done.20, f32[3,8,32,128]{3,1,2,0:T(8,128)S(1)} %get-tuple-element.32, f32[1,8,32,128]{3,1,2,0:T(8,128)S(1)} %copy-done.19, f32[5,8,128,32]{2,1,3,0:T(8,128)} %copy.122, f32[5,8,32,128]{3,1,2,0:T(8,128)} %fusion.71, ...), kind=kOutput, calls=%fused_computation.21 | convolution fusion | flops 33259520 | bytes 4588032 | tf_op jit(solution)/shard_map/il,flab->fiab/dot_general | solution.py:135
  (66 shorter events, 9.7 us)
Async XLA Ops:
  4.7 95.6 %copy-start = (f32[8,32,128]{2,0,1:T(8,128)}, f32[8,32,128]{2,0,1:T(8,128)S(1)}, u32[]{:S(2)}) copy-start(f32[8,32,128]{2,0,1:T(8,128)S(1)} %get-tuple-element.19) | copy-start | bytes 393220
  10.2 22.4 %all-to-all-start = ((f32[16,1,8192]{2,1,0:T(1,128)}), f32[16,1,8192]{2,1,0:T(1,128)S(1)}, u32[]{:S(2)}, u32[]{:S(2)}) async-start(f32[16,1,8192]{2,1,0:T(1,128)} %reshape.16), calls=%async_computation | async-start | bytes 1048576 | tf_op jit(solution)/shard_map/all_to_all | solution.py:147
  21.2 47.6 %collective-permute-start = (f32[4,4,32,128]{3,1,2,0:T(4,128)}, f32[4,4,32,128]{3,1,2,0:T(4,128)}, u32[]{:S(2)}, u32[]{:S(2)}) collective-permute-start(f32[4,4,32,128]{3,1,2,0:T(4,128)} %get-tuple-element.26), channel_id=1, source_target_pairs={{0,16},{16,32},{32,48},{48,64},{64,80},{80,96},{96,112},{112,128},... | collective-permute-start | bytes 786440 | tf_op jit(solution)/shard_map/ppermute | solution.py:30
  23.2 45.7 %collective-permute-start.1 = (f32[4,4,32,128]{3,1,2,0:T(4,128)S(1)}, f32[4,4,32,128]{3,1,2,0:T(4,128)}, u32[]{:S(2)}, u32[]{:S(2)}) collective-permute-start(f32[4,4,32,128]{3,1,2,0:T(4,128)S(1)} %get-tuple-element.27), channel_id=1, source_target_pairs={{16,0},{32,16},{48,32},{64,48},{80,64},{96,80},{112,96},{128,112},... | collective-permute-start | bytes 786440 | tf_op jit(solution)/shard_map/ppermute | solution.py:31
  40.3 2.4 %copy-start.2 = (f32[512,512,1,1]{1,0,3,2:T(8,128)S(1)}, f32[512,512,1,1]{1,0,3,2:T(8,128)}, u32[]{:S(2)}) copy-start(f32[512,512,1,1]{1,0,3,2:T(8,128)} %constant.35) | copy-start | bytes 3145732
  51.2 16.2 %copy-start.21 = (f32[128,128,1,1]{1,0,3,2:T(8,128)S(1)}, f32[128,128,1,1]{1,0,3,2:T(8,128)}, u32[]{:S(2)}) copy-start(f32[128,128,1,1]{1,0,3,2:T(8,128)} %constant.34) | copy-start | bytes 196612
  58.5 10.3 %copy-start.23 = (f32[8,16,1,1]{1,0,3,2:T(8,128)S(1)}, f32[8,16,1,1]{1,0,3,2:T(8,128)}, u32[]{:S(2)}) copy-start(f32[8,16,1,1]{1,0,3,2:T(8,128)} %constant.33) | copy-start | bytes 1540
  58.5 19.4 %all-to-all-start.1 = ((f32[16,1,8192]{2,1,0:T(1,128)}), f32[16,1,8192]{2,1,0:T(1,128)S(1)}, u32[]{:S(2)}, u32[]{:S(2)}) async-start(f32[16,1,8192]{2,1,0:T(1,128)} %reshape.18), calls=%async_computation.1 | async-start | bytes 1048576 | tf_op jit(solution)/shard_map/all_to_all | solution.py:150
  93.0 5.4 %copy-start.16 = (f32[4,8,32,128]{3,1,2,0:T(8,128)S(1)}, f32[4,8,32,128]{3,1,2,0:T(8,128)}, u32[]{:S(2)}) copy-start(f32[4,8,32,128]{3,1,2,0:T(8,128)} %convolution_bitcast_fusion) | copy-start | bytes 1572868
  96.5 3.9 %copy-start.10 = (f32[8,32,128]{2,0,1:T(8,128)}, f32[8,32,128]{2,0,1:T(8,128)S(1)}, u32[]{:S(2)}) copy-start(f32[8,32,128]{2,0,1:T(8,128)S(1)} %get-tuple-element.13) | copy-start | bytes 393220
  96.5 3.9 %copy-start.9 = (f32[4,8,128,32]{2,1,3,0:T(8,128)S(1)}, f32[4,8,128,32]{2,1,3,0:T(8,128)}, u32[]{:S(2)}) copy-start(f32[4,8,128,32]{2,1,3,0:T(8,128)} %copy.108) | copy-start | bytes 1572868
  96.5 3.9 %copy-start.14 = (f32[8,32,128]{2,1,0:T(8,128)S(1)}, f32[8,32,128]{2,1,0:T(8,128)}, u32[]{:S(2)}) copy-start(f32[8,32,128]{2,1,0:T(8,128)} %param.8) | copy-start | bytes 393220
  98.4 2.9 %copy-start.4 = (f32[8,32,128]{2,0,1:T(8,128)}, f32[8,32,128]{2,0,1:T(8,128)S(1)}, u32[]{:S(2)}) copy-start(f32[8,32,128]{2,0,1:T(8,128)S(1)} %get-tuple-element.11) | copy-start | bytes 393220
  99.5 1.8 copy-start.12
  99.5 0.8 copy-start.17
  101.3 0.9 copy-start.7
  106.3 6.6 %copy-start.8 = (f32[5,8,32,128]{3,1,2,0:T(8,128)S(1)}, f32[5,8,32,128]{3,1,2,0:T(8,128)}, u32[]{:S(2)}) copy-start(f32[5,8,32,128]{3,1,2,0:T(8,128)} %copy-done.7) | copy-start | bytes 1966084
  106.3 17.3 %all-to-all-start.2 = ((f32[16,1,10240]{2,1,0:T(1,128)}), f32[16,1,10240]{2,1,0:T(1,128)S(1)}, u32[]{:S(2)}, u32[]{:S(2)}) async-start(f32[16,1,10240]{2,1,0:T(1,128)} %reshape.20), calls=%async_computation.2 | async-start | bytes 1310720 | tf_op jit(solution)/shard_map/all_to_all | solution.py:147
  131.7 2.6 %copy-start.3 = (f32[512,512,1,1]{1,0,3,2:T(8,128)S(1)}, f32[512,512,1,1]{1,0,3,2:T(8,128)}, u32[]{:S(2)}) copy-start(f32[512,512,1,1]{1,0,3,2:T(8,128)} %constant.35) | copy-start | bytes 3145732
  141.0 14.2 %copy-start.11 = (f32[8,32,128]{2,0,1:T(8,128)S(1)}, f32[8,32,128]{2,0,1:T(8,128)}, u32[]{:S(2)}) copy-start(f32[8,32,128]{2,0,1:T(8,128)} %copy-done.10) | copy-start | bytes 393220
  141.0 14.2 %copy-start.18 = (f32[5,8,32,128]{3,1,2,0:T(8,128)S(1)}, f32[5,8,32,128]{3,1,2,0:T(8,128)}, u32[]{:S(2)}) copy-start(f32[5,8,32,128]{3,1,2,0:T(8,128)} %bitcast_dynamic-update-slice_fusion.4) | copy-start | bytes 1966084
  141.0 21.9 %copy-start.1 = (f32[8,32,128]{2,0,1:T(8,128)S(1)}, f32[8,32,128]{2,0,1:T(8,128)}, u32[]{:S(2)}) copy-start(f32[8,32,128]{2,0,1:T(8,128)} %copy-done) | copy-start | bytes 393220
  141.0 21.9 %copy-start.5 = (f32[8,32,128]{2,0,1:T(8,128)S(1)}, f32[8,32,128]{2,0,1:T(8,128)}, u32[]{:S(2)}) copy-start(f32[8,32,128]{2,0,1:T(8,128)} %copy-done.4) | copy-start | bytes 393220
  141.0 21.9 %copy-start.6 = (f32[4,8,32,128]{3,1,2,0:T(8,128)S(1)}, f32[4,8,32,128]{3,1,2,0:T(8,128)}, u32[]{:S(2)}) copy-start(f32[4,8,32,128]{3,1,2,0:T(8,128)} %fusion.66) | copy-start | bytes 1572868
  141.0 21.9 %copy-start.13 = (f32[8,32,128]{2,0,1:T(8,128)S(1)}, f32[8,32,128]{2,0,1:T(8,128)}, u32[]{:S(2)}) copy-start(f32[8,32,128]{2,0,1:T(8,128)} %copy-done.12) | copy-start | bytes 393220
  141.0 21.9 %copy-start.15 = (f32[8,32,128]{2,1,0:T(8,128)S(1)}, f32[8,32,128]{2,1,0:T(8,128)}, u32[]{:S(2)}) copy-start(f32[8,32,128]{2,1,0:T(8,128)} %param.8) | copy-start | bytes 393220
  150.2 13.0 %copy-start.22 = (f32[128,128,1,1]{1,0,3,2:T(8,128)S(1)}, f32[128,128,1,1]{1,0,3,2:T(8,128)}, u32[]{:S(2)}) copy-start(f32[128,128,1,1]{1,0,3,2:T(8,128)} %constant.34) | copy-start | bytes 196612
  150.2 19.8 %all-to-all-start.3 = ((f32[16,1,10240]{2,1,0:T(1,128)}), f32[16,1,10240]{2,1,0:T(1,128)S(1)}, u32[]{:S(2)}, u32[]{:S(2)}) async-start(f32[16,1,10240]{2,1,0:T(1,128)} %reshape.22), calls=%async_computation.3 | async-start | bytes 1310720 | tf_op jit(solution)/shard_map/all_to_all | solution.py:150
  155.2 35.8 %collective-permute-start.2 = (f32[5,4,32,128]{3,1,2,0:T(4,128)}, f32[5,4,32,128]{3,1,2,0:T(4,128)}, u32[]{:S(2)}, u32[]{:S(2)}) collective-permute-start(f32[5,4,32,128]{3,1,2,0:T(4,128)} %get-tuple-element.24), channel_id=1, source_target_pairs={{0,16},{16,32},{32,48},{48,64},{64,80},{80,96},{96,112},{112,128},... | collective-permute-start | bytes 983048 | tf_op jit(solution)/shard_map/ppermute | solution.py:30
  157.2 33.9 %collective-permute-start.3 = (f32[5,4,32,128]{3,1,2,0:T(4,128)}, f32[5,4,32,128]{3,1,2,0:T(4,128)}, u32[]{:S(2)}, u32[]{:S(2)}) collective-permute-start(f32[5,4,32,128]{3,1,2,0:T(4,128)} %get-tuple-element.25), channel_id=1, source_target_pairs={{16,0},{32,16},{48,32},{64,48},{80,64},{96,80},{112,96},{128,112},... | collective-permute-start | bytes 983048 | tf_op jit(solution)/shard_map/ppermute | solution.py:31
  189.2 1.9 copy-start.19
  189.2 1.8 copy-start.20
where the time goes:
time: 200 us; the launch traced here: 196 us
  local copies, waits for them, and re-layouts  91.3 us (46%)
  starting transfers between devices  47.4 us (24%)
  other arithmetic  24.1 us (12%)
  waiting for transfers between devices  21.4 us (11%)
  matrix products  10.7 us (5%)
    unnamed x60, local copies, waits for them, and re-layouts  46.2 us
    ppermute x2, starting transfers between devices, padded(): after = lax.ppermute(initial, axis, down)  15.2 us
    all_to_all x2, starting transfers between devices, derive_span(): lax.all_to_all(values, 'gy', split_axis=3, concat_axis=2, tiled=True)  15.1 us
    all_to_all x4, local copies, waits for them, and re-layouts, derive_span(): lax.all_to_all(derived, 'gy', split_axis=3, concat_axis=2, tiled=True)  15 us
    all_to_all x2, starting transfers between devices, derive_span(): lax.all_to_all(derived, 'gy', split_axis=3, concat_axis=2, tiled=True)  13.2 us
    dot_general x2, local copies, waits for them, and re-layouts, derive_span(): derived = jnp.einsum('fack,jk->facj', lines, z_matrix, precision=highest)  12.9 us
    all_to_all x2, waiting for transfers between devices, derive_span(): lax.all_to_all(derived, 'gy', split_axis=3, concat_axis=2, tiled=True)  11.6 us
    all_to_all x5, local copies, waits for them, and re-layouts, derive_span(): lax.all_to_all(values, 'gy', split_axis=3, concat_axis=2, tiled=True)  11.1 us
  transfers between devices with their start and end apart: 8, of which 3 were waited for; matrix products, arithmetic and copies ran while one was open for 28% of the time, Pallas kernels for 0%

commit v1 on v0

v1 whole, which is shorter than its diff:
```python
import jax
import jax.numpy as jnp
import ml_dtypes
import numpy as np
from jax import lax
from jax.experimental import pallas as pl
from jax.experimental.pallas import tpu as pltpu
from jax.sharding import PartitionSpec as P

CX = 8
CY = 8
NZ = 512
NY = 128
HALO = 4
GY = 16
ZB = NZ // GY
HZ = ZB // 2
MESH = pl.DeviceIdType.MESH

heat_ratio = 1.4
shear_resistance_reference = 0.08
sutherland_power_law = 0.7
prandtl = 0.72
section_step = 0.05
compact_alpha = 1.0 / 3.0
compact_near = 14.0 / 9.0
compact_far = 1.0 / 9.0
conduction = heat_ratio / ((heat_ratio - 1.0) * prandtl)


def tridiagonal_inverse_product(length, stencil):
    solved = np.array(stencil)
    upper_ratio = np.zeros(length)
    for row_index in range(length):
        if row_index == 0:
            pivot_value = 1.0
            solved[row_index] = solved[row_index] / pivot_value
        else:
            pivot_value = 1.0 - compact_alpha * upper_ratio[row_index - 1]
            solved[row_index] = (
                solved[row_index] - compact_alpha * solved[row_index - 1]
            ) / pivot_value
        upper_ratio[row_index] = compact_alpha / pivot_value
    for row_index in range(length - 2, -1, -1):
        solved[row_index] = solved[row_index] - upper_ratio[row_index] * solved[row_index + 1]
    return solved


def compact_matrix(block_size, margin):
    length = block_size + 2 * margin
    stencil = compact_near / 2.0 * (np.eye(length, k=1) - np.eye(length, k=-1))
    stencil = stencil + compact_far / 4.0 * (np.eye(length, k=2) - np.eye(length, k=-2))
    inverse_product = tridiagonal_inverse_product(length, stencil)
    return inverse_product[margin : margin + block_size]


def pitch_matrix(total, block_size):
    matrix = compact_matrix(block_size, HALO)
    result = np.zeros((total, total))
    rows_all = np.arange(total)
    block_start = rows_all // block_size * block_size
    for offset in range(block_size + 2 * HALO):
        columns = (block_start - HALO + offset) % total
        result[rows_all, columns] += matrix[rows_all % block_size, offset]
    return result


def span_kernel(offsets, total):
    angles = np.pi * offsets / total
    signs = np.where(offsets % 2 == 0, 1.0, -1.0)
    zero = offsets % total == 0
    sines = np.where(zero, 1.0, np.sin(angles))
    return np.where(zero, 0.0, np.pi / total * signs * np.cos(angles) / sines)


def high_low(matrix):
    high = matrix.astype(ml_dtypes.bfloat16)
    low = (matrix - high.astype(np.float64)).astype(ml_dtypes.bfloat16)
    return high, low


def span_operand():
    z = (np.arange(GY)[:, None] * ZB + np.arange(HZ)[None, :]).reshape(-1)
    near = span_kernel(z[:, None] - z[None, :], NZ)
    far = span_kernel(z[:, None] - (z[None, :] + HZ), NZ)
    return high_low(np.concatenate([near, far], 1))


def pitch_operand():
    high, low = high_low(pitch_matrix(NY, CY).T)
    top = np.concatenate([high, low], 1)
    bottom = np.concatenate([high, np.zeros_like(low)], 1)
    return np.concatenate([top, bottom], 0)


MATRIX_X = compact_matrix(CX, HALO)


def split(value):
    high = value.astype(jnp.bfloat16)
    return high, (value - high.astype(jnp.float32)).astype(jnp.bfloat16)


def compact_rows(segment):
    even = [segment[i] + segment[15 - i] for i in range(8)]
    odd = [segment[i] - segment[15 - i] for i in range(8)]
    result = [None] * 8
    for i in range(4):
        both = sum(float(0.5 * (MATRIX_X[i, j] - MATRIX_X[i, 15 - j])) * odd[j] for j in range(8))
        diff = sum(float(0.5 * (MATRIX_X[i, j] + MATRIX_X[i, 15 - j])) * even[j] for j in range(8))
        result[i] = both + diff
        result[7 - i] = both - diff
    return result


def exchange_halves(top, bottom, low_lanes):
    moved = pltpu.roll(jnp.where(low_lanes, bottom, top), NY // 2, axis=1)
    return jnp.where(low_lanes, top, moved), jnp.where(low_lanes, moved, bottom)


def viscosity(temperature):
    return shear_resistance_reference * jnp.exp(sutherland_power_law * jnp.log(temperature))


def kernel(
    rho_hbm, mom_hbm, en_hbm, dh_hbm, dl_hbm, yc_hbm, out_ref,
    con, dh, dl, yc, prim, halo_lo, halo_hi, flux_lo, flux_hi,
    a1_send, a1_recv, a2_send, a2_recv, b1_send, b1_recv, b2_send, b2_recv,
    grad_x, grad_y, flux_x, pitch_in, span_x, rhs_h, rhs_l, dz_t,
    load_sem, a2a_send_sem, a2a_recv_sem, halo_send_sem, halo_recv_sem,
):
    gx = lax.axis_index("gx")
    me = lax.axis_index("gy")
    n_gx = lax.axis_size("gx")
    right, left = lax.rem(gx + 1, n_gx), lax.rem(gx + n_gx - 1, n_gx)

    loads = [
        pltpu.make_async_copy(rho_hbm, con.at[0], load_sem.at[0]),
        pltpu.make_async_copy(mom_hbm, con.at[pl.ds(1, 3)], load_sem.at[1]),
        pltpu.make_async_copy(en_hbm, con.at[4], load_sem.at[2]),
        pltpu.make_async_copy(yc_hbm, yc, load_sem.at[3]),
        pltpu.make_async_copy(dh_hbm, dh, load_sem.at[4]),
        pltpu.make_async_copy(dl_hbm, dl, load_sem.at[5]),
    ]
    for copy in loads:
        copy.start()

    barrier = pltpu.get_barrier_semaphore()

    def greet(k, carry):
        pl.semaphore_signal(
            barrier, inc=1, device_id={"gy": lax.rem(me + k, GY)}, device_id_type=MESH
        )
        return carry

    lax.fori_loop(1, GY, greet, 0)
    for neighbour in (left, right):
        pl.semaphore_signal(barrier, inc=1, device_id={"gx": neighbour}, device_id_type=MESH)

    low_lanes = lax.broadcasted_iota(jnp.int32, (HZ, NY), 1) < NY // 2

    def a2a(phase, send, recv, k):
        return pltpu.make_async_remote_copy(
            src_ref=send.at[lax.rem(me + k, GY)],
            dst_ref=recv.at[me],
            send_sem=a2a_send_sem.at[phase, k],
            recv_sem=a2a_recv_sem.at[phase, k],
            device_id={"gy": lax.rem(me + k, GY)},
            device_id_type=MESH,
        )

    def a2a_start(phase, send, recv):
        def body(k, carry):
            a2a(phase, send, recv, k).start()
            return carry

        lax.fori_loop(1, GY, body, 0)
        recv[me] = send[me]

    def a2a_wait_recv(phase, send, recv):
        def body(k, carry):
            a2a(phase, send, recv, k).wait_recv()
            return carry

        lax.fori_loop(1, GY, body, 0)

    def a2a_wait_send(phase, send, recv):
        def body(k, carry):
            a2a(phase, send, recv, k).wait_send()
            return carry

        lax.fori_loop(1, GY, body, 0)

    def halo_pair(source, lo, hi, slot):
        up = pltpu.make_async_remote_copy(
            src_ref=source.at[pl.ds(CX - HALO, HALO)], dst_ref=lo,
            send_sem=halo_send_sem.at[0, slot], recv_sem=halo_recv_sem.at[0, slot],
            device_id={"gx": right}, device_id_type=MESH,
        )
        down = pltpu.make_async_remote_copy(
            src_ref=source.at[pl.ds(0, HALO)], dst_ref=hi,
            send_sem=halo_send_sem.at[1, slot], recv_sem=halo_recv_sem.at[1, slot],
            device_id={"gx": left}, device_id_type=MESH,
        )
        return up, down

    for copy in loads[:3]:
        copy.wait()

    def first(x, carry):
        values = [con[f, x] for f in range(5)]
        for f in range(5):
            p0, p1 = exchange_halves(values[f][:HZ], values[f][HZ:], low_lanes)
            a1_send[2 * x, f] = p0
            a1_send[2 * x + 1, f] = p1
        inverse = 1.0 / values[0]
        speeds = [values[1 + i] * inverse for i in range(3)]
        kinetic = 0.5 * (
            values[1] * speeds[0] + values[2] * speeds[1] + values[3] * speeds[2]
        )
        temperature = (heat_ratio - 1.0) * (values[4] - kinetic) * inverse
        for f, value in enumerate(speeds + [temperature]):
            prim[f, x] = value
            high, low = split(value)
            rows = pl.ds(pl.multiple_of(x * ZB, ZB), ZB)
            pitch_in[f, rows, :NY] = high
            pitch_in[f, rows, NY:] = low
        return carry

    lax.fori_loop(0, CX, first, 0)

    pl.semaphore_wait(barrier, GY + 1)

    sources = [prim.at[0], prim.at[1], prim.at[2], prim.at[3], con.at[1]]
    halos = [halo_pair(sources[f], halo_lo.at[f], halo_hi.at[f], f) for f in range(5)]
    for f in (2, 0, 1, 3, 4):
        for copy in halos[f]:
            copy.start()
    a2a_start(0, a1_send, a1_recv)

    loads[3].wait()

    def pitch_derivative(f):
        product = jnp.dot(pitch_in[f], yc[...], preferred_element_type=jnp.float32)
        return (product[:, :NY] + product[:, NY:]).reshape(CX, ZB, NY)

    for f in range(4):
        grad_y[f] = pitch_derivative(f)

    def stream_derivative(own, lo, hi, emit):
        def body(t, carry):
            rows = pl.ds(pl.multiple_of(t * 8, 8), 8)
            segment = [lo[i, rows] for i in range(HALO)]
            segment += [own[i, rows] for i in range(CX)]
            segment += [hi[i, rows] for i in range(HALO)]
            for i, value in enumerate(compact_rows(segment)):
                emit(i, rows, value)
            return carry

        lax.fori_loop(0, ZB // 8, body, 0)

    def halo_wait(copies):
        for copy in copies:
            copy.wait_recv()

    def prim_x(f):
        halo_wait(halos[f])

        def emit(i, rows, value):
            grad_x[f, i, rows] = value

        stream_derivative(sources[f], halo_lo.at[f], halo_hi.at[f], emit)

    prim_x(2)
    prim_x(0)

    def extras(x, carry):
        values = [grad_x[2, x], grad_y[2, x], grad_x[0, x] + grad_y[1, x]]
        for f in range(3):
            p0, p1 = exchange_halves(values[f][:HZ], values[f][HZ:], low_lanes)
            a2_send[2 * x, f] = p0
            a2_send[2 * x + 1, f] = p1
        return carry

    lax.fori_loop(0, CX, extras, 0)
    a2a_start(1, a2_send, a2_recv)
    prim_x(1)
    prim_x(3)

    for copy in loads[4:]:
        copy.wait()
    a2a_wait_recv(0, a1_send, a1_recv)

    def span_first(s, carry):
        density, m1, m2, m3, energy = [a1_recv[s, f] for f in range(5)]
        inverse = 1.0 / density
        v1, v2, v3 = m1 * inverse, m2 * inverse, m3 * inverse
        kinetic = 0.5 * (m1 * v1 + m2 * v2 + m3 * v3)
        span_x[4, s] = (heat_ratio - 1.0) * (energy - kinetic) * inverse
        span_x[0, s] = v1
        span_x[1, s] = v2
        span_x[2, s] = v3
        span_x[3, s] = m3
        return carry

    lax.fori_loop(0, GY, span_first, 0, unroll=2)

    def build(fields):
        def body(s, carry):
            after = lax.rem(s + 1, GY)
            near_rows = pl.ds(pl.multiple_of(s * HZ, HZ), HZ)
            far_rows = pl.ds(pl.multiple_of(NZ // 2 + s * HZ, HZ), HZ)
            for f in fields:
                columns = pl.ds(f * NY, NY)
                here = span_x[f, s]
                other = pltpu.roll(
                    jnp.where(low_lanes, span_x[f, after], here), NY // 2, axis=1
                )
                high, low = split(here)
                rhs_h[near_rows, columns] = high
                rhs_l[near_rows, columns] = low
                high, low = split(other)
                rhs_h[far_rows, columns] = high
                rhs_l[far_rows, columns] = low
            return carry

        lax.fori_loop(0, GY, body, 0, unroll=2)

    def span_product(start, count):
        columns = pl.ds(start * NY, count * NY)
        high = rhs_h[:, columns]
        product = jnp.dot(dh[...], high, preferred_element_type=jnp.float32)
        product += jnp.dot(dh[...], rhs_l[:, columns], preferred_element_type=jnp.float32)
        product += jnp.dot(dl[...], high, preferred_element_type=jnp.float32)
        return product

    build(range(4))
    for pair in (0, 2):
        product = span_product(pair, 2)
        for f in range(2):
            b1_send[:, pair + f] = product[:, f * NY : (f + 1) * NY].reshape(GY, HZ, NY)
    a2a_start(2, b1_send, b1_recv)
    build([4])
    dz_t[...] = span_product(4, 1).reshape(GY, HZ, NY)

    a2a_wait_recv(1, a2_send, a2_recv)

    def span_second(s, carry):
        m1, m2, m3, energy = [a1_recv[s, f] for f in range(1, 5)]
        v1, v2, v3, temperature = [span_x[f, s] for f in (0, 1, 2, 4)]
        pressure = temperature * a1_recv[s, 0]
        dz1, dz2, dz3 = [b1_send[s, f] for f in range(3)]
        dx3, dy3, plane = [a2_recv[s, f] for f in range(3)]
        visc = viscosity(temperature)
        s13 = visc * (dz1 + dx3)
        s23 = visc * (dz2 + dy3)
        s33 = visc * (2.0 * dz3 - (2.0 / 3.0) * (plane + dz3))
        work = s13 * v1 + s23 * v2 + s33 * v3
        span_x[5, s] = m1 * v3 - s13
        span_x[6, s] = m2 * v3 - s23
        span_x[7, s] = m3 * v3 - s33 + pressure
        span_x[8, s] = (energy + pressure) * v3 - work - (visc * conduction) * dz_t[s]
        return carry

    lax.fori_loop(0, GY, span_second, 0, unroll=2)
    build(range(5, 9))
    for pair in (0, 2):
        product = span_product(5 + pair, 2)
        for f in range(2):
            b2_send[:, pair + f] = product[:, f * NY : (f + 1) * NY].reshape(GY, HZ, NY)
    a2a_start(3, b2_send, b2_recv)

    a2a_wait_recv(2, b1_send, b1_recv)

    def fluxes(x, carry):
        dz = []
        for f in range(4):
            top, bottom = exchange_halves(b1_recv[2 * x, f], b1_recv[2 * x + 1, f], low_lanes)
            dz.append(jnp.concatenate([top, bottom], 0))
        out_ref[0, x] = dz[3]
        density, m1, m2, m3, energy = [con[f, x] for f in range(5)]
        v1, v2, v3, temperature = [prim[f, x] for f in range(4)]
        pressure = temperature * density
        dx1, dx2, dx3, dxt = [grad_x[f, x] for f in range(4)]
        dy1, dy2, dy3, dyt = [grad_y[f, x] for f in range(4)]
        dz1, dz2, dz3 = dz[:3]
        visc = viscosity(temperature)
        heat = visc * conduction
        bulk = (2.0 / 3.0) * (dx1 + dy2 + dz3)
        total = energy + pressure
        s11 = visc * (2.0 * dx1 - bulk)
        s22 = visc * (2.0 * dy2 - bulk)
        s12 = visc * (dx2 + dy1)
        s13 = visc * (dx3 + dz1)
        s23 = visc * (dy3 + dz2)
        flux_x[0, x] = m1 * v1 + pressure - s11
        flux_x[1, x] = m2 * v1 - s12
        flux_x[2, x] = m3 * v1 - s13
        flux_x[3, x] = total * v1 - (s11 * v1 + s12 * v2 + s13 * v3) - heat * dxt
        pitch = [
            m2,
            m1 * v2 - s12,
            m2 * v2 + pressure - s22,
            m3 * v2 - s23,
            total * v2 - (s12 * v1 + s22 * v2 + s23 * v3) - heat * dyt,
        ]
        rows = pl.ds(pl.multiple_of(x * ZB, ZB), ZB)
        for f in range(5):
            high, low = split(pitch[f])
            pitch_in[f, rows, :NY] = high
            pitch_in[f, rows, NY:] = low
        return carry

    lax.fori_loop(0, CX, fluxes, 0)

    flux_halos = [
        halo_pair(flux_x.at[f], flux_lo.at[f], flux_hi.at[f], 5 + f) for f in range(4)
    ]
    for copies in flux_halos:
        for copy in copies:
            copy.start()

    out_ref[0] += pitch_derivative(0)
    for f in range(1, 5):
        out_ref[f] = pitch_derivative(f)

    def accumulate(f, own, lo, hi):
        def emit(i, rows, value):
            out_ref[f, i, rows] += value

        stream_derivative(own, lo, hi, emit)

    halo_wait(halos[4])
    accumulate(0, con.at[1], halo_lo.at[4], halo_hi.at[4])
    for f in range(4):
        halo_wait(flux_halos[f])
        accumulate(1 + f, flux_x.at[f], flux_lo.at[f], flux_hi.at[f])

    a2a_wait_recv(3, b2_send, b2_recv)

    def last(x, carry):
        for f in range(4):
            top, bottom = exchange_halves(b2_recv[2 * x, f], b2_recv[2 * x + 1, f], low_lanes)
            out_ref[1 + f, x] += jnp.concatenate([top, bottom], 0)
        return carry

    lax.fori_loop(0, CX, last, 0)

    a2a_wait_send(0, a1_send, a1_recv)
    a2a_wait_send(1, a2_send, a2_recv)
    a2a_wait_send(2, b1_send, b1_recv)
    a2a_wait_send(3, b2_send, b2_recv)
    for copies in halos + flux_halos:
        for copy in copies:
            copy.wait_send()


def per_device(mass_per_volume, momentum, energy):
    dh, dl = span_operand()
    yc = pitch_operand()
    f32, bf16 = jnp.float32, jnp.bfloat16
    field = (CX, ZB, NY)
    piece = (HZ, NY)
    spread = pl.pallas_call(
        kernel,
        out_shape=jax.ShapeDtypeStruct((5,) + field, f32),
        in_specs=[pl.BlockSpec(memory_space=pl.ANY)] * 6,
        out_specs=pl.BlockSpec(memory_space=pltpu.VMEM),
        scratch_shapes=[
            pltpu.VMEM((5,) + field, f32),
            pltpu.VMEM((NZ // 2, NZ), bf16),
            pltpu.VMEM((NZ // 2, NZ), bf16),
            pltpu.VMEM((2 * NY, 2 * NY), bf16),
            pltpu.VMEM((4,) + field, f32),
            pltpu.VMEM((5, HALO, ZB, NY), f32),
            pltpu.VMEM((5, HALO, ZB, NY), f32),
            pltpu.VMEM((4, HALO, ZB, NY), f32),
            pltpu.VMEM((4, HALO, ZB, NY), f32),
            pltpu.VMEM((GY, 5) + piece, f32),
            pltpu.VMEM((GY, 5) + piece, f32),
            pltpu.VMEM((GY, 3) + piece, f32),
            pltpu.VMEM((GY, 3) + piece, f32),
            pltpu.VMEM((GY, 4) + piece, f32),
            pltpu.VMEM((GY, 4) + piece, f32),
            pltpu.VMEM((GY, 4) + piece, f32),
            pltpu.VMEM((GY, 4) + piece, f32),
            pltpu.VMEM((4,) + field, f32),
            pltpu.VMEM((4,) + field, f32),
            pltpu.VMEM((4,) + field, f32),
            pltpu.VMEM((5, CX * ZB, 2 * NY), bf16),
            pltpu.VMEM((9, GY) + piece, f32),
            pltpu.VMEM((NZ, 9 * NY), bf16),
            pltpu.VMEM((NZ, 9 * NY), bf16),
            pltpu.VMEM((GY,) + piece, f32),
            pltpu.SemaphoreType.DMA((6,)),
            pltpu.SemaphoreType.DMA((4, GY)),
            pltpu.SemaphoreType.DMA((4, GY)),
            pltpu.SemaphoreType.DMA((2, 9)),
            pltpu.SemaphoreType.DMA((2, 9)),
        ],
        compiler_params=pltpu.CompilerParams(collective_id=0, has_side_effects=True),
    )(mass_per_volume, momentum, energy, jnp.asarray(dh), jnp.asarray(dl), jnp.asarray(yc))
    conserved = jnp.concatenate([mass_per_volume[None], momentum, energy[None]], 0)
    tendency = -spread
    return tendency, conserved + section_step * tendency


def solution(mesh):
    in_specs = (P("gx", "gy", None), P(None, "gx", "gy", None), P("gx", "gy", None))
    out_specs = (P(None, "gx", "gy", None), P(None, "gx", "gy", None))
    return jax.shard_map(
        per_device, mesh=mesh, in_specs=in_specs, out_specs=out_specs, check_vma=False
    )
```

time: 200 us -> 63.3 us (0.32); the launches traced: 196 us -> 63.1 us
  local copies, waits for them, and re-layouts: 91.3 us -> 0.01 us
  Pallas kernels: 0 us -> 60.1 us
  starting transfers between devices: 47.4 us -> 0 us
  other arithmetic: 24.1 us -> 2.34 us
  waiting for transfers between devices: 21.4 us -> 0 us
  matrix products: 10.7 us -> 0 us
    pallas_call x0 -> x1, Pallas kernels: none -> 60.1 us  [per_device(): pl.pallas_call(kernel, out_shape=jax.ShapeDtypeStruct((5,) + field, f32),...]
    unnamed x60 -> x6, local copies, waits for them, and re-layouts: 46.2 us -> 0.01 us
    all_to_all x4 -> x0, starting transfers between devices: 28.3 us -> none  [the longest x2 15.1 us: derive_span(): lax.all_to_all(values, 'gy', split_axis=3, concat_axis=2, tiled=True)]
    all_to_all x9 -> x0, local copies, waits for them, and re-layouts: 26.1 us -> none  [the longest x4 15 us: derive_span(): lax.all_to_all(derived, 'gy', split_axis=3, concat_axis=2, tiled=True)]
    all_to_all x4 -> x0, waiting for transfers between devices: 21.3 us -> none  [the longest x2 11.6 us: derive_span(): lax.all_to_all(derived, 'gy', split_axis=3, concat_axis=2, tiled=True)]
    ppermute x4 -> x0, starting transfers between devices: 19 us -> none  [the longest x2 15.2 us: padded(): after = lax.ppermute(initial, axis, down)]
    dot_general x2 -> x0, local copies, waits for them, and re-layouts: 12.9 us -> none  [derive_span(): derived = jnp.einsum('fack,jk->facj', lines, z_matrix, precision=highest)]
    dot_general x6 -> x0, matrix products: 10.7 us -> none  [the longest x2 5.49 us: apply_x(): return jnp.einsum('il,flab->fiab', x_matrix, extended, precision=highest)]
  transfers between devices with their start and end apart: 8 -> 0, of which waited for: 3 -> 0; matrix products, arithmetic and copies ran while one was open for 28% -> 0% of each run, Pallas kernels for 0% -> 0%
where the time goes in v1:
time: 63.3 us; the launch traced here: 63.1 us
  Pallas kernels  60.1 us (95%)
  other arithmetic  2.34 us (4%)
  between operations  0.69 us (1%)
    pallas_call x1, Pallas kernels, per_device(): pl.pallas_call(kernel, out_shape=jax.ShapeDtypeStruct((5,) + field, f32),...  60.1 us
    add x1, other arithmetic, per_device(): return (tendency, conserved + section_step * tendency)  2.34 us

profile of v1, /device:TPU:1, one launch (start us, length us, event | category | flops | bytes accessed | tf_op | source)
XLA Modules:
  0.0 63.1 jit_solution(321059342983216265)
XLA Ops:
  0.6 0.0 copy-start
  0.6 0.0 copy-start.1
  0.6 0.0 copy-start.2
  0.7 60.1 %shard_map.77 = f32[5,8,32,128]{3,2,1,0:T(8,128)} custom-call(f32[8,32,128]{2,1,0:T(8,128)} %rho_hbm.1, f32[3,8,32,128]{3,2,1,0:T(8,128)} %mom_hbm.1, f32[8,32,128]{2,1,0:T(8,128)} %en_hbm.1, bf16[256,512]{1,0:T(8,128)(2,1)} %constant.8.clone.dh_hbm, bf16[256,512]{1,0:T(8,128)(2,1)} %constant.9.clone.dl_hbm, bf16[256,256]{1,0:T(8,128)(2,1)} %constant.10.clone.yc_hbm), custom_call_target="tpu_custom_call" | custom-call | tf_op jit(solution)/shard_map/pallas_call | solution.py:464
  60.8 0.0 copy-done
  60.8 0.0 copy-done.1
  60.8 0.0 copy-done.2
  60.8 2.3 %maximum_add_fusion = (f32[5,8,32,128]{3,2,1,0:T(8,128)}, f32[5,8,32,128]{3,2,1,0:T(8,128)}) fusion(f32[1,8,32,128]{3,2,1,0:T(8,128)S(1)} %bitcast.2, f32[3,8,32,128]{3,2,1,0:T(8,128)S(1)} %copy-done, f32[1,8,32,128]{3,2,1,0:T(8,128)S(1)} %bitcast.3, f32[5,8,32,128]{3,2,1,0:T(8,128)} %shard_map.77), kind=kLoop, calls=%fused_computation | loop fusion | flops 819200 | bytes 2621440 | tf_op jit(solution)/shard_map/add | solution.py:505
Async XLA Ops:
  0.6 60.1 %copy-start = (f32[3,8,32,128]{3,2,1,0:T(8,128)S(1)}, f32[3,8,32,128]{3,2,1,0:T(8,128)}, u32[]{:S(2)}) copy-start(f32[3,8,32,128]{3,2,1,0:T(8,128)} %mom_hbm.1) | copy-start | bytes 1179652
  0.6 60.1 %copy-start.1 = (f32[8,32,128]{2,1,0:T(8,128)S(1)}, f32[8,32,128]{2,1,0:T(8,128)}, u32[]{:S(2)}) copy-start(f32[8,32,128]{2,1,0:T(8,128)} %en_hbm.1) | copy-start | bytes 393220
  0.6 60.1 %copy-start.2 = (f32[8,32,128]{2,1,0:T(8,128)S(1)}, f32[8,32,128]{2,1,0:T(8,128)}, u32[]{:S(2)}) copy-start(f32[8,32,128]{2,1,0:T(8,128)} %rho_hbm.1) | copy-start | bytes 393220

commit v2 on v1

v2 whole, which is shorter than its diff:
```python
import jax
import jax.numpy as jnp
import ml_dtypes
import numpy as np
from jax import lax
from jax.experimental import pallas as pl
from jax.experimental.pallas import tpu as pltpu
from jax.sharding import PartitionSpec as P

CX = 8
CY = 8
NZ = 512
NY = 128
HALO = 4
GY = 16
ZB = NZ // GY
HZ = ZB // 2
MESH = pl.DeviceIdType.MESH

heat_ratio = 1.4
shear_resistance_reference = 0.08
sutherland_power_law = 0.7
prandtl = 0.72
section_step = 0.05
compact_alpha = 1.0 / 3.0
compact_near = 14.0 / 9.0
compact_far = 1.0 / 9.0
conduction = heat_ratio / ((heat_ratio - 1.0) * prandtl)


def tridiagonal_inverse_product(length, stencil):
    solved = np.array(stencil)
    upper_ratio = np.zeros(length)
    for row_index in range(length):
        if row_index == 0:
            pivot_value = 1.0
            solved[row_index] = solved[row_index] / pivot_value
        else:
            pivot_value = 1.0 - compact_alpha * upper_ratio[row_index - 1]
            solved[row_index] = (
                solved[row_index] - compact_alpha * solved[row_index - 1]
            ) / pivot_value
        upper_ratio[row_index] = compact_alpha / pivot_value
    for row_index in range(length - 2, -1, -1):
        solved[row_index] = solved[row_index] - upper_ratio[row_index] * solved[row_index + 1]
    return solved


def compact_matrix(block_size, margin):
    length = block_size + 2 * margin
    stencil = compact_near / 2.0 * (np.eye(length, k=1) - np.eye(length, k=-1))
    stencil = stencil + compact_far / 4.0 * (np.eye(length, k=2) - np.eye(length, k=-2))
    inverse_product = tridiagonal_inverse_product(length, stencil)
    return inverse_product[margin : margin + block_size]


def pitch_matrix(total, block_size):
    matrix = compact_matrix(block_size, HALO)
    result = np.zeros((total, total))
    rows_all = np.arange(total)
    block_start = rows_all // block_size * block_size
    for offset in range(block_size + 2 * HALO):
        columns = (block_start - HALO + offset) % total
        result[rows_all, columns] += matrix[rows_all % block_size, offset]
    return result


def span_kernel(offsets, total):
    angles = np.pi * offsets / total
    signs = np.where(offsets % 2 == 0, 1.0, -1.0)
    zero = offsets % total == 0
    sines = np.where(zero, 1.0, np.sin(angles))
    return np.where(zero, 0.0, np.pi / total * signs * np.cos(angles) / sines)


def high_low(matrix):
    high = matrix.astype(ml_dtypes.bfloat16)
    low = (matrix - high.astype(np.float64)).astype(ml_dtypes.bfloat16)
    return high, low


def span_operand():
    z = (np.arange(GY)[:, None] * ZB + np.arange(HZ)[None, :]).reshape(-1)
    near = span_kernel(z[:, None] - z[None, :], NZ)
    far = span_kernel(z[:, None] - (z[None, :] + HZ), NZ)
    return high_low(np.concatenate([near, far], 1))


def pitch_operand():
    high, low = high_low(pitch_matrix(NY, CY).T)
    top = np.concatenate([high, low], 1)
    bottom = np.concatenate([high, np.zeros_like(low)], 1)
    return np.concatenate([top, bottom], 0)


MATRIX_X = compact_matrix(CX, HALO)


def split(value):
    high = value.astype(jnp.bfloat16)
    return high, (value - high.astype(jnp.float32)).astype(jnp.bfloat16)


def compact_rows(segment):
    even = [segment[i] + segment[15 - i] for i in range(8)]
    odd = [segment[i] - segment[15 - i] for i in range(8)]
    result = [None] * 8
    for i in range(4):
        both = sum(float(0.5 * (MATRIX_X[i, j] - MATRIX_X[i, 15 - j])) * odd[j] for j in range(8))
        diff = sum(float(0.5 * (MATRIX_X[i, j] + MATRIX_X[i, 15 - j])) * even[j] for j in range(8))
        result[i] = both + diff
        result[7 - i] = both - diff
    return result


def exchange_halves(top, bottom, low_lanes):
    moved = pltpu.roll(jnp.where(low_lanes, bottom, top), NY // 2, axis=1)
    return jnp.where(low_lanes, top, moved), jnp.where(low_lanes, moved, bottom)


def viscosity(temperature):
    return shear_resistance_reference * jnp.exp(sutherland_power_law * jnp.log(temperature))


STEPS = [
    (dx, dy, dc)
    for dc in range(2)
    for dx, dy in ((2, 1), (1, 1), (3, 1), (2, 0), (0, 1), (1, 0), (3, 0))
] + [(0, 0, 1)]


def kernel(
    rho_hbm, mom_hbm, en_hbm, dh_hbm, dl_hbm, yc_hbm, out_ref, con,
    dh, dl, yc, prim, halo_lo, halo_hi, flux_lo, flux_hi,
    speed_send, speed_recv, state_send, state_recv, cross_send, cross_recv,
    slope_send, slope_recv, slope2_send, slope2_recv, div_send, div_recv,
    grad_x, grad_y, flux_x, keep, pitch_in, span_x, rhs_h, rhs_l, dz_t, span_visc,
    load_sem, a2a_send_sem, a2a_recv_sem, halo_send_sem, halo_recv_sem,
):
    gx = lax.axis_index("gx")
    me = lax.axis_index("gy")
    n_gx = lax.axis_size("gx")
    right, left = lax.rem(gx + 1, n_gx), lax.rem(gx + n_gx - 1, n_gx)
    chip_x, chip_y, core = me // 4, lax.rem(me // 2, 2), lax.rem(me, 2)
    partners = [
        lax.rem(chip_x + dx, 4) * 4 + lax.rem(chip_y + dy, 2) * 2 + lax.rem(core + dc, 2)
        for dx, dy, dc in STEPS
    ]

    loads = [
        pltpu.make_async_copy(rho_hbm, con.at[0], load_sem.at[0]),
        pltpu.make_async_copy(mom_hbm, con.at[pl.ds(1, 3)], load_sem.at[1]),
        pltpu.make_async_copy(en_hbm, con.at[4], load_sem.at[2]),
        pltpu.make_async_copy(yc_hbm, yc, load_sem.at[3]),
        pltpu.make_async_copy(dh_hbm, dh, load_sem.at[4]),
        pltpu.make_async_copy(dl_hbm, dl, load_sem.at[5]),
    ]
    for copy in loads:
        copy.start()

    barrier = pltpu.get_barrier_semaphore()
    for partner in partners:
        pl.semaphore_signal(barrier, inc=1, device_id={"gy": partner}, device_id_type=MESH)
    for neighbour in (left, right):
        pl.semaphore_signal(barrier, inc=1, device_id={"gx": neighbour}, device_id_type=MESH)

    low_lanes = lax.broadcasted_iota(jnp.int32, (HZ, NY), 1) < NY // 2

    def a2a(phase, send, recv, step, partner):
        return pltpu.make_async_remote_copy(
            src_ref=send.at[partner],
            dst_ref=recv.at[me],
            send_sem=a2a_send_sem.at[phase, step],
            recv_sem=a2a_recv_sem.at[phase, step],
            device_id={"gy": partner},
            device_id_type=MESH,
        )

    def a2a_start(phase, send, recv):
        for step, partner in enumerate(partners):
            a2a(phase, send, recv, step, partner).start()
        recv[me] = send[me]

    def a2a_wait_recv(phase, send, recv):
        def body(step, carry):
            a2a(phase, send, recv, step, partners[0]).wait_recv()
            return carry

        lax.fori_loop(0, GY - 1, body, 0)

    def a2a_wait_send(phase, send, recv):
        def body(step, carry):
            a2a(phase, send, recv, step, partners[0]).wait_send()
            return carry

        lax.fori_loop(0, GY - 1, body, 0)

    def halo_pair(source, lo, hi, slot):
        up = pltpu.make_async_remote_copy(
            src_ref=source.at[pl.ds(CX - HALO, HALO)], dst_ref=lo,
            send_sem=halo_send_sem.at[0, slot], recv_sem=halo_recv_sem.at[0, slot],
            device_id={"gx": right}, device_id_type=MESH,
        )
        down = pltpu.make_async_remote_copy(
            src_ref=source.at[pl.ds(0, HALO)], dst_ref=hi,
            send_sem=halo_send_sem.at[1, slot], recv_sem=halo_recv_sem.at[1, slot],
            device_id={"gx": left}, device_id_type=MESH,
        )
        return up, down

    def pack(send, slot, x, value):
        p0, p1 = exchange_halves(value[:HZ], value[HZ:], low_lanes)
        send[2 * x, slot] = p0
        send[2 * x + 1, slot] = p1

    def unpack(recv, slot, x):
        top, bottom = exchange_halves(recv[2 * x, slot], recv[2 * x + 1, slot], low_lanes)
        return jnp.concatenate([top, bottom], 0)

    def pitch_store(f, x, value):
        high, low = split(value)
        rows = pl.ds(pl.multiple_of(x * ZB, ZB), ZB)
        pitch_in[f, rows, :NY] = high
        pitch_in[f, rows, NY:] = low

    for copy in loads[:3]:
        copy.wait()

    def first(x, carry):
        density, m1, m2, m3, energy = [con[f, x] for f in range(5)]
        inverse = 1.0 / density
        v1, v2, v3 = m1 * inverse, m2 * inverse, m3 * inverse
        kinetic = 0.5 * (m1 * v1 + m2 * v2 + m3 * v3)
        temperature = (heat_ratio - 1.0) * (energy - kinetic) * inverse
        pack(speed_send, 0, x, v1)
        pack(speed_send, 1, x, v3)
        pack(state_send, 0, x, v2)
        pack(state_send, 1, x, density)
        pack(state_send, 2, x, temperature)
        for f, value in enumerate((v1, v2, v3, temperature)):
            prim[f, x] = value
            pitch_store(f, x, value)
        keep[0, x] = viscosity(temperature)
        return carry

    lax.fori_loop(0, CX, first, 0)

    pl.semaphore_wait(barrier, GY + 1)

    sources = [prim.at[0], prim.at[1], prim.at[2], prim.at[3], con.at[1]]
    halos = [halo_pair(sources[f], halo_lo.at[f], halo_hi.at[f], f) for f in range(5)]
    for f in (2, 0):
        for copy in halos[f]:
            copy.start()
    a2a_start(0, speed_send, speed_recv)
    a2a_start(1, state_send, state_recv)
    for f in (1, 3, 4):
        for copy in halos[f]:
            copy.start()

    loads[3].wait()

    def pitch_derivative(f):
        product = jnp.dot(pitch_in[f], yc[...], preferred_element_type=jnp.float32)
        return (product[:, :NY] + product[:, NY:]).reshape(CX, ZB, NY)

    for f in range(4):
        grad_y[f] = pitch_derivative(f)

    def stream_derivative(own, lo, hi, emit):
        def body(t, carry):
            rows = pl.ds(pl.multiple_of(t * 8, 8), 8)
            segment = [lo[i, rows] for i in range(HALO)]
            segment += [own[i, rows] for i in range(CX)]
            segment += [hi[i, rows] for i in range(HALO)]
            for i, value in enumerate(compact_rows(segment)):
                emit(i, rows, value)
            return carry

        lax.fori_loop(0, ZB // 8, body, 0)

    def halo_wait(copies):
        for copy in copies:
            copy.wait_recv()

    def prim_x(f):
        halo_wait(halos[f])

        def emit(i, rows, value):
            grad_x[f, i, rows] = value

        stream_derivative(sources[f], halo_lo.at[f], halo_hi.at[f], emit)

    prim_x(2)
    prim_x(0)

    def extras(x, carry):
        pack(cross_send, 0, x, grad_x[2, x])
        pack(cross_send, 1, x, grad_y[2, x])
        pack(cross_send, 2, x, grad_x[0, x] + grad_y[1, x])
        return carry

    lax.fori_loop(0, CX, extras, 0)
    a2a_start(2, cross_send, cross_recv)

    def build(fields):
        def body(s, carry):
            after = lax.rem(s + 1, GY)
            near_rows = pl.ds(pl.multiple_of(s * HZ, HZ), HZ)
            far_rows = pl.ds(pl.multiple_of(NZ // 2 + s * HZ, HZ), HZ)
            for column, fetch in fields:
                columns = pl.ds(column * NY, NY)
                here = fetch(s)
                other = pltpu.roll(jnp.where(low_lanes, fetch(after), here), NY // 2, axis=1)
                high, low = split(here)
                rhs_h[near_rows, columns] = high
                rhs_l[near_rows, columns] = low
                high, low = split(other)
                rhs_h[far_rows, columns] = high
                rhs_l[far_rows, columns] = low
            return carry

        lax.fori_loop(0, GY, body, 0, unroll=2)

    def span_product(start, count):
        columns = pl.ds(start * NY, count * NY)
        high = rhs_h[:, columns]
        product = jnp.dot(dh[...], high, preferred_element_type=jnp.float32)
        product += jnp.dot(dh[...], rhs_l[:, columns], preferred_element_type=jnp.float32)
        product += jnp.dot(dl[...], high, preferred_element_type=jnp.float32)
        return [
            product[:, f * NY : (f + 1) * NY].reshape(GY, HZ, NY) for f in range(count)
        ]

    for copy in loads[4:]:
        copy.wait()
    a2a_wait_recv(0, speed_send, speed_recv)
    build([(0, lambda s: speed_recv[s, 0]), (1, lambda s: speed_recv[s, 1])])
    for f, value in enumerate(span_product(0, 2)):
        slope_send[:, f] = value
    a2a_start(3, slope_send, slope_recv)

    a2a_wait_recv(1, state_send, state_recv)

    def span_first(s, carry):
        span_x[0, s] = state_recv[s, 1] * speed_recv[s, 1]
        span_visc[s] = viscosity(state_recv[s, 2])
        return carry

    lax.fori_loop(0, GY, span_first, 0, unroll=2)
    build([(2, lambda s: state_recv[s, 0]), (3, lambda s: span_x[0, s])])
    for f, value in enumerate(span_product(2, 2)):
        slope2_send[:, f] = value
    a2a_start(4, slope2_send, slope2_recv)
    build([(4, lambda s: state_recv[s, 2])])
    dz_t[...] = span_product(4, 1)[0]

    prim_x(1)
    prim_x(3)

    a2a_wait_recv(2, cross_send, cross_recv)

    def span_second(s, carry):
        v1, v3 = speed_recv[s, 0], speed_recv[s, 1]
        v2, density, temperature = [state_recv[s, f] for f in range(3)]
        m3 = span_x[0, s]
        pressure = temperature * density
        enthalpy = (heat_ratio / (heat_ratio - 1.0)) * pressure + 0.5 * density * (
            v1 * v1 + v2 * v2 + v3 * v3
        )
        dz1, dz3, dz2 = slope_send[s, 0], slope_send[s, 1], slope2_send[s, 0]
        dx3, dy3, plane = [cross_recv[s, f] for f in range(3)]
        visc = span_visc[s]
        s13 = visc * (dz1 + dx3)
        s23 = visc * (dz2 + dy3)
        s33 = visc * (2.0 * dz3 - (2.0 / 3.0) * (plane + dz3))
        work = s13 * v1 + s23 * v2 + s33 * v3
        span_x[1, s] = m3 * v1 - s13
        span_x[2, s] = m3 * v2 - s23
        span_x[3, s] = m3 * v3 - s33 + pressure
        span_x[4, s] = enthalpy * v3 - work - (visc * conduction) * dz_t[s]
        return carry

    lax.fori_loop(0, GY, span_second, 0, unroll=2)
    build([(5 + f, lambda s, f=f: span_x[1 + f, s]) for f in range(4)])
    for pair in (0, 2):
        for f, value in enumerate(span_product(5 + pair, 2)):
            div_send[:, pair + f] = value
    a2a_start(5, div_send, div_recv)

    a2a_wait_recv(3, slope_send, slope_recv)

    def stream_flux(x, carry):
        dz1, dz3 = unpack(slope_recv, 0, x), unpack(slope_recv, 1, x)
        density, m1, m2, m3, energy = [con[f, x] for f in range(5)]
        v1, v2, v3, temperature = [prim[f, x] for f in range(4)]
        pressure = temperature * density
        dx1, dx2, dx3, dxt = [grad_x[f, x] for f in range(4)]
        visc = keep[0, x]
        bulk = (2.0 / 3.0) * (dx1 + grad_y[1, x] + dz3)
        s11 = visc * (2.0 * dx1 - bulk)
        s12 = visc * (dx2 + grad_y[0, x])
        s13 = visc * (dx3 + dz1)
        flux_x[0, x] = m1 * v1 + pressure - s11
        flux_x[1, x] = m2 * v1 - s12
        flux_x[2, x] = m3 * v1 - s13
        work = s11 * v1 + s12 * v2 + s13 * v3
        flux_x[3, x] = (energy + pressure) * v1 - work - (visc * conduction) * dxt
        keep[1, x] = bulk
        keep[2, x] = s12
        return carry

    lax.fori_loop(0, CX, stream_flux, 0)
    flux_halos = [
        halo_pair(flux_x.at[f], flux_lo.at[f], flux_hi.at[f], 5 + f) for f in range(4)
    ]
    for copies in flux_halos:
        for copy in copies:
            copy.start()

    a2a_wait_recv(4, slope2_send, slope2_recv)

    def pitch_flux(x, carry):
        dz2 = unpack(slope2_recv, 0, x)
        out_ref[0, x] = unpack(slope2_recv, 1, x)
        density, m1, m2, m3, energy = [con[f, x] for f in range(5)]
        v1, v2, v3, temperature = [prim[f, x] for f in range(4)]
        pressure = temperature * density
        visc, bulk, s12 = [keep[f, x] for f in range(3)]
        s22 = visc * (2.0 * grad_y[1, x] - bulk)
        s23 = visc * (grad_y[2, x] + dz2)
        work = s12 * v1 + s22 * v2 + s23 * v3
        pitch_store(0, x, m2)
        pitch_store(1, x, m1 * v2 - s12)
        pitch_store(2, x, m2 * v2 + pressure - s22)
        pitch_store(3, x, m3 * v2 - s23)
        flux = (energy + pressure) * v2 - work - (visc * conduction) * grad_y[3, x]
        pitch_store(4, x, flux)
        return carry

    lax.fori_loop(0, CX, pitch_flux, 0)
    out_ref[0] += pitch_derivative(0)
    for f in range(1, 5):
        out_ref[f] = pitch_derivative(f)

    def accumulate(f, own, lo, hi):
        def emit(i, rows, value):
            out_ref[f, i, rows] += value

        stream_derivative(own, lo, hi, emit)

    halo_wait(halos[4])
    accumulate(0, con.at[1], halo_lo.at[4], halo_hi.at[4])
    for f in range(4):
        halo_wait(flux_halos[f])
        accumulate(1 + f, flux_x.at[f], flux_lo.at[f], flux_hi.at[f])

    a2a_wait_recv(5, div_send, div_recv)

    def last(x, carry):
        for f in range(4):
            out_ref[1 + f, x] += unpack(div_recv, f, x)
        return carry

    lax.fori_loop(0, CX, last, 0)

    a2a_wait_send(0, speed_send, speed_recv)
    a2a_wait_send(1, state_send, state_recv)
    a2a_wait_send(2, cross_send, cross_recv)
    a2a_wait_send(3, slope_send, slope_recv)
    a2a_wait_send(4, slope2_send, slope2_recv)
    a2a_wait_send(5, div_send, div_recv)
    for copies in halos + flux_halos:
        for copy in copies:
            copy.wait_send()


def per_device(mass_per_volume, momentum, energy):
    dh, dl = span_operand()
    yc = pitch_operand()
    f32, bf16 = jnp.float32, jnp.bfloat16
    field = (CX, ZB, NY)
    piece = (HZ, NY)
    spread, conserved = pl.pallas_call(
        kernel,
        out_shape=[jax.ShapeDtypeStruct((5,) + field, f32)] * 2,
        in_specs=[pl.BlockSpec(memory_space=pltpu.HBM)] * 6,
        out_specs=[pl.BlockSpec(memory_space=pltpu.VMEM)] * 2,
        scratch_shapes=[
            pltpu.VMEM((NZ // 2, NZ), bf16),
            pltpu.VMEM((NZ // 2, NZ), bf16),
            pltpu.VMEM((2 * NY, 2 * NY), bf16),
            pltpu.VMEM((4,) + field, f32),
            pltpu.VMEM((5, HALO, ZB, NY), f32),
            pltpu.VMEM((5, HALO, ZB, NY), f32),
            pltpu.VMEM((4, HALO, ZB, NY), f32),
            pltpu.VMEM((4, HALO, ZB, NY), f32),
        ]
        + [pltpu.VMEM((GY, n) + piece, f32) for n in (2, 3, 3, 2, 2, 4) for _ in range(2)]
        + [
            pltpu.VMEM((4,) + field, f32),
            pltpu.VMEM((4,) + field, f32),
            pltpu.VMEM((4,) + field, f32),
            pltpu.VMEM((3,) + field, f32),
            pltpu.VMEM((5, CX * ZB, 2 * NY), bf16),
            pltpu.VMEM((5, GY) + piece, f32),
            pltpu.VMEM((NZ, 9 * NY), bf16),
            pltpu.VMEM((NZ, 9 * NY), bf16),
            pltpu.VMEM((GY,) + piece, f32),
            pltpu.VMEM((GY,) + piece, f32),
            pltpu.SemaphoreType.DMA((6,)),
            pltpu.SemaphoreType.DMA((6, GY - 1)),
            pltpu.SemaphoreType.DMA((6, GY - 1)),
            pltpu.SemaphoreType.DMA((2, 9)),
            pltpu.SemaphoreType.DMA((2, 9)),
        ],
        compiler_params=pltpu.CompilerParams(
            collective_id=0, has_side_effects=True, vmem_limit_bytes=24 * 1024 * 1024
        ),
    )(*[pltpu.with_memory_space_constraint(x, pltpu.HBM) for x in (mass_per_volume, momentum, energy, jnp.asarray(dh), jnp.asarray(dl), jnp.asarray(yc))])
    tendency = -spread
    return tendency, conserved + section_step * tendency


def solution(mesh):
    in_specs = (P("gx", "gy", None), P(None, "gx", "gy", None), P("gx", "gy", None))
    out_specs = (P(None, "gx", "gy", None), P(None, "gx", "gy", None))
    return jax.shard_map(
        per_device, mesh=mesh, in_specs=in_specs, out_specs=out_specs, check_vma=False
    )
```

time: 63.3 us -> 58.6 us (0.926)
  Pallas kernels: 60.1 us -> 56.5 us
  other arithmetic: 2.34 us -> 1.25 us
    pallas_call x1, Pallas kernels: 60.1 us -> 56.5 us  [per_device(): pl.pallas_call(kernel, out_shape=[jax.ShapeDtypeStruct((5,) + field, f32)...]
    add x1, other arithmetic: 2.34 us -> 1.25 us  [per_device(): return (tendency, conserved + section_step * tendency)]
where the time goes in v2:
time: 58.6 us; the launch traced here: 58.4 us
  Pallas kernels  56.5 us (96%)
  other arithmetic  1.25 us (2%)
  between operations  0.64 us (1%)
    pallas_call x1, Pallas kernels, per_device(): pl.pallas_call(kernel, out_shape=[jax.ShapeDtypeStruct((5,) + field, f32)...  56.5 us
    add x1, other arithmetic, per_device(): return (tendency, conserved + section_step * tendency)  1.25 us

profile of v2, /device:TPU:1, one launch (start us, length us, event | category | flops | bytes accessed | tf_op | source)
XLA Modules:
  0.0 58.4 jit_solution(16986847366147212343)
XLA Ops:
  0.6 56.5 %shard_map.77 = (f32[5,8,32,128]{3,2,1,0:T(8,128)S(1)}, f32[5,8,32,128]{3,2,1,0:T(8,128)S(1)}) custom-call(f32[8,32,128]{2,1,0:T(8,128)} %rho_hbm.1, f32[3,8,32,128]{3,2,1,0:T(8,128)} %mom_hbm.1, f32[8,32,128]{2,1,0:T(8,128)} %en_hbm.1, bf16[256,512]{1,0:T(8,128)(2,1)} %constant.8.clone.dh_hbm, bf16[256,512]{1,0:T(8,128)(2,1)} %constant.9.clone.dl_hbm, ...), custom_call_target="tpu_custom_call" | custom-call | tf_op jit(solution)/shard_map/pallas_call | solution.py:484
  57.2 1.3 %multiply_add_fusion = (f32[5,8,32,128]{3,2,1,0:T(8,128)}, f32[5,8,32,128]{3,2,1,0:T(8,128)}) fusion(f32[5,8,32,128]{3,2,1,0:T(8,128)S(1)} %get-tuple-element.5, f32[5,8,32,128]{3,2,1,0:T(8,128)S(1)} %get-tuple-element.4), kind=kLoop, calls=%fused_computation | loop fusion | flops 491520 | bytes 2621440 | tf_op jit(solution)/shard_map/add | solution.py:522

commit v3 on v2

--- a/solution.py
+++ b/solution.py
@@ -93,7 +93,21 @@
     return np.concatenate([top, bottom], 0)
 
 
+def half_pitch_operand():
+    matrix = pitch_matrix(NY, CY).T
+    half = NY // 2
+    near, far = matrix[:half, :half], matrix[half:, :half]
+    assert np.allclose(near, matrix[half:, half:]) and np.allclose(far, matrix[:half, half:])
+    stacked = np.concatenate([np.kron(np.eye(2), near), np.kron(np.eye(2), far)], 0)
+    return np.concatenate(high_low(stacked), 1)
+
+
 MATRIX_X = compact_matrix(CX, HALO)
+EDGE = HALO - 1
+OUTERMOST = float(MATRIX_X[0, 0] / MATRIX_X[0, 1])
+assert np.allclose(MATRIX_X[:, 0], OUTERMOST * MATRIX_X[:, 1], rtol=1e-9, atol=1e-12)
+SEGMENT = CX + 2 * EDGE
+MATRIX_E = MATRIX_X[:, 1:-1]
 
 
 def split(value):
@@ -102,14 +116,16 @@
 
 
 def compact_rows(segment):
-    even = [segment[i] + segment[15 - i] for i in range(8)]
-    odd = [segment[i] - segment[15 - i] for i in range(8)]
-    result = [None] * 8
-    for i in range(4):
-        both = sum(float(0.5 * (MATRIX_X[i, j] - MATRIX_X[i, 15 - j])) * odd[j] for j in range(8))
-        diff = sum(float(0.5 * (MATRIX_X[i, j] + MATRIX_X[i, 15 - j])) * even[j] for j in range(8))
+    half, end = SEGMENT // 2, SEGMENT - 1
+    even = [segment[i] + segment[end - i] for i in range(half)]
+    odd = [segment[i] - segment[end - i] for i in range(half)]
+    result = [None] * CX
+    for i in range(CX // 2):
+        row = MATRIX_E[i]
+        both = sum(float(0.5 * (row[j] - row[end - j])) * odd[j] for j in range(half))
+        diff = sum(float(0.5 * (row[j] + row[end - j])) * even[j] for j in range(half))
         result[i] = both + diff
-        result[7 - i] = both - diff
+        result[CX - 1 - i] = both - diff
     return result
 
 
@@ -130,11 +146,12 @@
 
 
 def kernel(
-    rho_hbm, mom_hbm, en_hbm, dh_hbm, dl_hbm, yc_hbm, out_ref, con,
-    dh, dl, yc, prim, halo_lo, halo_hi, flux_lo, flux_hi,
+    rho_hbm, mom_hbm, en_hbm, dh_hbm, dl_hbm, yc_hbm, ys_hbm, out_ref, con,
+    dh, dl, yc, ys, prim, edges, halo_lo, halo_hi, flux_lo, flux_hi,
     speed_send, speed_recv, state_send, state_recv, cross_send, cross_recv,
     slope_send, slope_recv, slope2_send, slope2_recv, div_send, div_recv,
     grad_x, grad_y, flux_x, keep, pitch_in, span_x, rhs_h, rhs_l, dz_t, span_visc,
+    sib_value, sib_send_buf, span_in, span_dy, dz_v2, sib_send_sem, sib_recv_sem,
     load_sem, a2a_send_sem, a2a_recv_sem, halo_send_sem, halo_recv_sem,
 ):
     gx = lax.axis_index("gx")
@@ -154,11 +171,13 @@
         pltpu.make_async_copy(yc_hbm, yc, load_sem.at[3]),
         pltpu.make_async_copy(dh_hbm, dh, load_sem.at[4]),
         pltpu.make_async_copy(dl_hbm, dl, load_sem.at[5]),
+        pltpu.make_async_copy(ys_hbm, ys, load_sem.at[6]),
     ]
     for copy in loads:
         copy.start()
 
     barrier = pltpu.get_barrier_semaphore()
+    sibling = partners[-1]
     for partner in partners:
         pl.semaphore_signal(barrier, inc=1, device_id={"gy": partner}, device_id_type=MESH)
     for neighbour in (left, right):
@@ -195,18 +214,33 @@
 
         lax.fori_loop(0, GY - 1, body, 0)
 
-    def halo_pair(source, lo, hi, slot):
+    def halo_pair(lo, hi, slot):
         up = pltpu.make_async_remote_copy(
-            src_ref=source.at[pl.ds(CX - HALO, HALO)], dst_ref=lo,
+            src_ref=edges.at[slot, 0], dst_ref=lo,
             send_sem=halo_send_sem.at[0, slot], recv_sem=halo_recv_sem.at[0, slot],
             device_id={"gx": right}, device_id_type=MESH,
         )
         down = pltpu.make_async_remote_copy(
-            src_ref=source.at[pl.ds(0, HALO)], dst_ref=hi,
+            src_ref=edges.at[slot, 1], dst_ref=hi,
             send_sem=halo_send_sem.at[1, slot], recv_sem=halo_recv_sem.at[1, slot],
             device_id={"gx": left}, device_id_type=MESH,
         )
         return up, down
+
+    def edge_store(source, slot):
+        edges[slot, 0, 0] = source[CX - 3] + OUTERMOST * source[CX - 4]
+        edges[slot, 0, 1] = source[CX - 2]
+        edges[slot, 0, 2] = source[CX - 1]
+        edges[slot, 1, 0] = source[0]
+        edges[slot, 1, 1] = source[1]
+        edges[slot, 1, 2] = source[2] + OUTERMOST * source[3]
+
+    def sibling_copy(source, slot):
+        return pltpu.make_async_remote_copy(
+            src_ref=source, dst_ref=sib_value.at[slot],
+            send_sem=sib_send_sem.at[slot], recv_sem=sib_recv_sem.at[slot],
+            device_id={"gy": sibling}, device_id_type=MESH,
+        )
 
     def pack(send, slot, x, value):
         p0, p1 = exchange_halves(value[:HZ], value[HZ:], low_lanes)
@@ -245,16 +279,16 @@
 
     lax.fori_loop(0, CX, first, 0)
 
+    sources = [prim.at[0], prim.at[1], prim.at[2], prim.at[3], con.at[1]]
+    for f in range(5):
+        edge_store(sources[f], f)
+
     pl.semaphore_wait(barrier, GY + 1)
-
-    sources = [prim.at[0], prim.at[1], prim.at[2], prim.at[3], con.at[1]]
-    halos = [halo_pair(sources[f], halo_lo.at[f], halo_hi.at[f], f) for f in range(5)]
-    for f in (2, 0):
-        for copy in halos[f]:
-            copy.start()
     a2a_start(0, speed_send, speed_recv)
     a2a_start(1, state_send, state_recv)
-    for f in (1, 3, 4):
+
+    halos = [halo_pair(halo_lo.at[f], halo_hi.at[f], f) for f in range(5)]
+    for f in (2, 0, 1, 3, 4):
         for copy in halos[f]:
             copy.start()
 
@@ -264,15 +298,15 @@
         product = jnp.dot(pitch_in[f], yc[...], preferred_element_type=jnp.float32)
         return (product[:, :NY] + product[:, NY:]).reshape(CX, ZB, NY)
 
-    for f in range(4):
+    for f in (0, 1, 3):
         grad_y[f] = pitch_derivative(f)
 
     def stream_derivative(own, lo, hi, emit):
         def body(t, carry):
             rows = pl.ds(pl.multiple_of(t * 8, 8), 8)
-            segment = [lo[i, rows] for i in range(HALO)]
+            segment = [lo[i, rows] for i in range(EDGE)]
             segment += [own[i, rows] for i in range(CX)]
-            segment += [hi[i, rows] for i in range(HALO)]
+            segment += [hi[i, rows] for i in range(EDGE)]
             for i, value in enumerate(compact_rows(segment)):
                 emit(i, rows, value)
             return carry
@@ -296,8 +330,7 @@
 
     def extras(x, carry):
         pack(cross_send, 0, x, grad_x[2, x])
-        pack(cross_send, 1, x, grad_y[2, x])
-        pack(cross_send, 2, x, grad_x[0, x] + grad_y[1, x])
+        pack(cross_send, 1, x, grad_x[0, x])
         return carry
 
     lax.fori_loop(0, CX, extras, 0)
@@ -334,13 +367,31 @@
 
     for copy in loads[4:]:
         copy.wait()
+    def half_pitch_derivative(fetch, slot):
+        def body(s, carry):
+            rows = pl.ds(pl.multiple_of(s * HZ, HZ), HZ)
+            for side, value in enumerate((fetch(s), sib_value[slot, s])):
+                high, low = split(value)
+                span_in[0, rows, side * NY : (side + 1) * NY] = high
+                span_in[1, rows, side * NY : (side + 1) * NY] = low
+            return carry
+
+        lax.fori_loop(0, GY, body, 0, unroll=2)
+        product = jnp.dot(span_in[0], ys[...], preferred_element_type=jnp.float32)
+        rest = jnp.dot(span_in[1], ys[:, :NY], preferred_element_type=jnp.float32)
+        return (product[:, :NY] + product[:, NY:] + rest).reshape(GY, HZ, NY)
+
     a2a_wait_recv(0, speed_send, speed_recv)
+    siblings = [sibling_copy(speed_recv.at[:, 1], 0), sibling_copy(state_recv.at[:, 0], 1)]
+    siblings += [sibling_copy(sib_send_buf.at[f], 2 + f) for f in range(2)]
+    siblings[0].start()
     build([(0, lambda s: speed_recv[s, 0]), (1, lambda s: speed_recv[s, 1])])
     for f, value in enumerate(span_product(0, 2)):
         slope_send[:, f] = value
     a2a_start(3, slope_send, slope_recv)
 
     a2a_wait_recv(1, state_send, state_recv)
+    siblings[1].start()
 
     def span_first(s, carry):
         span_x[0, s] = state_recv[s, 1] * speed_recv[s, 1]
@@ -349,11 +400,31 @@
 
     lax.fori_loop(0, GY, span_first, 0, unroll=2)
     build([(2, lambda s: state_recv[s, 0]), (3, lambda s: span_x[0, s])])
-    for f, value in enumerate(span_product(2, 2)):
-        slope2_send[:, f] = value
+    slopes = span_product(2, 2)
+    dz_v2[...] = slopes[0]
+    slope2_send[:, 0] = slopes[1]
     a2a_start(4, slope2_send, slope2_recv)
+
+    siblings[0].wait_recv()
+    span_dy[0] = half_pitch_derivative(lambda s: speed_recv[s, 1], 0)
+
+    def shear(s, carry):
+        s23 = span_visc[s] * (dz_v2[s] + span_dy[0, s])
+        sib_send_buf[0, s] = s23
+        sib_send_buf[1, s] = s23 * speed_recv[s, 1]
+        return carry
+
+    lax.fori_loop(0, GY, shear, 0, unroll=2)
+    for copy in siblings[2:]:
+        copy.start()
+    siblings[1].wait_recv()
+    span_dy[1] = half_pitch_derivative(lambda s: state_recv[s, 0], 1)
     build([(4, lambda s: state_recv[s, 2])])
     dz_t[...] = span_product(4, 1)[0]
+
+    for f in range(2):
+        siblings[2 + f].wait_recv()
+        span_dy[2 + f] = half_pitch_derivative(lambda s, f=f: sib_send_buf[f, s], 2 + f)
 
     prim_x(1)
     prim_x(3)
@@ -368,11 +439,11 @@
         enthalpy = (heat_ratio / (heat_ratio - 1.0)) * pressure + 0.5 * density * (
             v1 * v1 + v2 * v2 + v3 * v3
         )
-        dz1, dz3, dz2 = slope_send[s, 0], slope_send[s, 1], slope2_send[s, 0]
-        dx3, dy3, plane = [cross_recv[s, f] for f in range(3)]
+        dz1, dz3 = slope_send[s, 0], slope_send[s, 1]
+        dx3, plane = cross_recv[s, 0], cross_recv[s, 1] + span_dy[1, s]
         visc = span_visc[s]
         s13 = visc * (dz1 + dx3)
-        s23 = visc * (dz2 + dy3)
+        s23 = sib_send_buf[0, s]
         s33 = visc * (2.0 * dz3 - (2.0 / 3.0) * (plane + dz3))
         work = s13 * v1 + s23 * v2 + s33 * v3
         span_x[1, s] = m3 * v1 - s13
@@ -385,7 +456,7 @@
     build([(5 + f, lambda s, f=f: span_x[1 + f, s]) for f in range(4)])
     for pair in (0, 2):
         for f, value in enumerate(span_product(5 + pair, 2)):
-            div_send[:, pair + f] = value
+            div_send[:, pair + f] = value - span_dy[pair + f] if pair else value
     a2a_start(5, div_send, div_recv)
 
     a2a_wait_recv(3, slope_send, slope_recv)
@@ -411,29 +482,26 @@
         return carry
 
     lax.fori_loop(0, CX, stream_flux, 0)
-    flux_halos = [
-        halo_pair(flux_x.at[f], flux_lo.at[f], flux_hi.at[f], 5 + f) for f in range(4)
-    ]
-    for copies in flux_halos:
-        for copy in copies:
+    flux_halos = [halo_pair(flux_lo.at[f], flux_hi.at[f], 5 + f) for f in range(4)]
+    for f in range(4):
+        edge_store(flux_x.at[f], 5 + f)
+        for copy in flux_halos[f]:
             copy.start()
 
     a2a_wait_recv(4, slope2_send, slope2_recv)
 
     def pitch_flux(x, carry):
-        dz2 = unpack(slope2_recv, 0, x)
-        out_ref[0, x] = unpack(slope2_recv, 1, x)
+        out_ref[0, x] = unpack(slope2_recv, 0, x)
         density, m1, m2, m3, energy = [con[f, x] for f in range(5)]
         v1, v2, v3, temperature = [prim[f, x] for f in range(4)]
         pressure = temperature * density
         visc, bulk, s12 = [keep[f, x] for f in range(3)]
         s22 = visc * (2.0 * grad_y[1, x] - bulk)
-        s23 = visc * (grad_y[2, x] + dz2)
-        work = s12 * v1 + s22 * v2 + s23 * v3
+        work = s12 * v1 + s22 * v2
         pitch_store(0, x, m2)
         pitch_store(1, x, m1 * v2 - s12)
         pitch_store(2, x, m2 * v2 + pressure - s22)
-        pitch_store(3, x, m3 * v2 - s23)
+        pitch_store(3, x, m3 * v2)
         flux = (energy + pressure) * v2 - work - (visc * conduction) * grad_y[3, x]
         pitch_store(4, x, flux)
         return carry
@@ -470,6 +538,8 @@
     a2a_wait_send(3, slope_send, slope_recv)
     a2a_wait_send(4, slope2_send, slope2_recv)
     a2a_wait_send(5, div_send, div_recv)
+    for copy in siblings:
+        copy.wait_send()
     for copies in halos + flux_halos:
         for copy in copies:
             copy.wait_send()
@@ -484,19 +554,21 @@
     spread, conserved = pl.pallas_call(
         kernel,
         out_shape=[jax.ShapeDtypeStruct((5,) + field, f32)] * 2,
-        in_specs=[pl.BlockSpec(memory_space=pltpu.HBM)] * 6,
+        in_specs=[pl.BlockSpec(memory_space=pltpu.HBM)] * 7,
         out_specs=[pl.BlockSpec(memory_space=pltpu.VMEM)] * 2,
         scratch_shapes=[
             pltpu.VMEM((NZ // 2, NZ), bf16),
             pltpu.VMEM((NZ // 2, NZ), bf16),
             pltpu.VMEM((2 * NY, 2 * NY), bf16),
+            pltpu.VMEM((2 * NY, 2 * NY), bf16),
             pltpu.VMEM((4,) + field, f32),
-            pltpu.VMEM((5, HALO, ZB, NY), f32),
-            pltpu.VMEM((5, HALO, ZB, NY), f32),
-            pltpu.VMEM((4, HALO, ZB, NY), f32),
-            pltpu.VMEM((4, HALO, ZB, NY), f32),
+            pltpu.VMEM((9, 2, EDGE, ZB, NY), f32),
+            pltpu.VMEM((5, EDGE, ZB, NY), f32),
+            pltpu.VMEM((5, EDGE, ZB, NY), f32),
+            pltpu.VMEM((4, EDGE, ZB, NY), f32),
+            pltpu.VMEM((4, EDGE, ZB, NY), f32),
         ]
-        + [pltpu.VMEM((GY, n) + piece, f32) for n in (2, 3, 3, 2, 2, 4) for _ in range(2)]
+        + [pltpu.VMEM((GY, n) + piece, f32) for n in (2, 3, 2, 2, 1, 4) for _ in range(2)]
         + [
             pltpu.VMEM((4,) + field, f32),
             pltpu.VMEM((4,) + field, f32),
@@ -508,7 +580,14 @@
             pltpu.VMEM((NZ, 9 * NY), bf16),
             pltpu.VMEM((GY,) + piece, f32),
             pltpu.VMEM((GY,) + piece, f32),
-            pltpu.SemaphoreType.DMA((6,)),
+            pltpu.VMEM((4, GY) + piece, f32),
+            pltpu.VMEM((2, GY) + piece, f32),
+            pltpu.VMEM((2, NZ // 2, 2 * NY), bf16),
+            pltpu.VMEM((4, GY) + piece, f32),
+            pltpu.VMEM((GY,) + piece, f32),
+            pltpu.SemaphoreType.DMA((4,)),
+            pltpu.SemaphoreType.DMA((4,)),
+            pltpu.SemaphoreType.DMA((7,)),
             pltpu.SemaphoreType.DMA((6, GY - 1)),
             pltpu.SemaphoreType.DMA((6, GY - 1)),
             pltpu.SemaphoreType.DMA((2, 9)),
@@ -517,7 +596,7 @@
         compiler_params=pltpu.CompilerParams(
             collective_id=0, has_side_effects=True, vmem_limit_bytes=24 * 1024 * 1024
         ),
-    )(*[pltpu.with_memory_space_constraint(x, pltpu.HBM) for x in (mass_per_volume, momentum, energy, jnp.asarray(dh), jnp.asarray(dl), jnp.asarray(yc))])
+    )(*[pltpu.with_memory_space_constraint(x, pltpu.HBM) for x in (mass_per_volume, momentum, energy, jnp.asarray(dh), jnp.asarray(dl), jnp.asarray(yc), jnp.asarray(half_pitch_operand()))])
     tendency = -spread
     return tendency, conserved + section_step * tendency
 

time: 58.6 us -> 54.2 us (0.925)
  Pallas kernels: 56.5 us -> 52.1 us
    pallas_call x1, Pallas kernels: 56.5 us -> 52.1 us  [per_device(): pl.pallas_call(kernel, out_shape=[jax.ShapeDtypeStruct((5,) + field, f32)...]
where the time goes in v3:
time: 54.2 us; the launch traced here: 54 us
  Pallas kernels  52.1 us (96%)
  other arithmetic  1.25 us (2%)
  between operations  0.64 us (1%)
    pallas_call x1, Pallas kernels, per_device(): pl.pallas_call(kernel, out_shape=[jax.ShapeDtypeStruct((5,) + field, f32)...  52.1 us
    add x1, other arithmetic, per_device(): return (tendency, conserved + section_step * tendency)  1.25 us

profile of v3, /device:TPU:1, one launch (start us, length us, event | category | flops | bytes accessed | tf_op | source)
XLA Modules:
  0.0 54.0 jit_solution(11437937531115373684)
XLA Ops:
  0.6 52.1 %shard_map.86 = (f32[5,8,32,128]{3,2,1,0:T(8,128)S(1)}, f32[5,8,32,128]{3,2,1,0:T(8,128)S(1)}) custom-call(f32[8,32,128]{2,1,0:T(8,128)} %rho_hbm.1, f32[3,8,32,128]{3,2,1,0:T(8,128)} %mom_hbm.1, f32[8,32,128]{2,1,0:T(8,128)} %en_hbm.1, bf16[256,512]{1,0:T(8,128)(2,1)} %constant.10.clone.dh_hbm, bf16[256,512]{1,0:T(8,128)(2,1)} %constant.11.clone.dl_hbm, ...), custom_call_target="tpu_custom_call" | custom-call | tf_op jit(solution)/shard_map/pallas_call | solution.py:554
  52.8 1.3 %multiply_add_fusion = (f32[5,8,32,128]{3,2,1,0:T(8,128)}, f32[5,8,32,128]{3,2,1,0:T(8,128)}) fusion(f32[5,8,32,128]{3,2,1,0:T(8,128)S(1)} %get-tuple-element.5, f32[5,8,32,128]{3,2,1,0:T(8,128)S(1)} %get-tuple-element.4), kind=kLoop, calls=%fused_computation | loop fusion | flops 491520 | bytes 2621440 | tf_op jit(solution)/shard_map/add | solution.py:601

commit v4 on v3

--- a/solution.py
+++ b/solution.py
@@ -138,6 +138,8 @@
     return shear_resistance_reference * jnp.exp(sutherland_power_law * jnp.log(temperature))
 
 
+RUN = 16
+RELAYED = (1, 3, 4, 7, 8)
 STEPS = [
     (dx, dy, dc)
     for dc in range(2)
@@ -152,7 +154,7 @@
     slope_send, slope_recv, slope2_send, slope2_recv, div_send, div_recv,
     grad_x, grad_y, flux_x, keep, pitch_in, span_x, rhs_h, rhs_l, dz_t, span_visc,
     sib_value, sib_send_buf, span_in, span_dy, dz_v2, sib_send_sem, sib_recv_sem,
-    load_sem, a2a_send_sem, a2a_recv_sem, halo_send_sem, halo_recv_sem,
+    load_sem, a2a_send_sem, a2a_recv_sem, halo_send_sem, halo_recv_sem, relay, relay_send_sem, relay_recv_sem,
 ):
     gx = lax.axis_index("gx")
     me = lax.axis_index("gy")
@@ -182,6 +184,16 @@
         pl.semaphore_signal(barrier, inc=1, device_id={"gy": partner}, device_id_type=MESH)
     for neighbour in (left, right):
         pl.semaphore_signal(barrier, inc=1, device_id={"gx": neighbour}, device_id_type=MESH)
+
+    run = lax.rem(gx, RUN)
+    first_in_run, last_in_run = run == 0, run == RUN - 1
+    relays_up, relays_down = run == 1, run == RUN - 2
+    beyond_right, beyond_left = lax.rem(gx + 2, n_gx), lax.rem(gx + n_gx - 2, n_gx)
+    for condition, source in ((relays_up, beyond_left), (relays_down, beyond_right)):
+
+        @pl.when(condition)
+        def _(source=source):
+            pl.semaphore_signal(barrier, inc=1, device_id={"gx": source}, device_id_type=MESH)
 
     low_lanes = lax.broadcasted_iota(jnp.int32, (HZ, NY), 1) < NY // 2
 
@@ -226,6 +238,56 @@
             device_id={"gx": left}, device_id_type=MESH,
         )
         return up, down
+
+    def halo_start(pair, slot):
+        sides = ((pair[0], last_in_run, beyond_right), (pair[1], first_in_run, beyond_left))
+        for side, (copy, at_end, target) in enumerate(sides):
+            if slot not in RELAYED:
+                copy.start()
+                continue
+
+            @pl.when(jnp.logical_not(at_end))
+            def _(copy=copy):
+                copy.start()
+
+            @pl.when(at_end)
+            def _(side=side, target=target):
+                pltpu.make_async_remote_copy(
+                    src_ref=edges.at[slot, side], dst_ref=relay.at[RELAYED.index(slot)],
+                    send_sem=halo_send_sem.at[side, slot],
+                    recv_sem=relay_recv_sem.at[RELAYED.index(slot)],
+                    device_id={"gx": target}, device_id_type=MESH,
+                ).start()
+
+    def relay_copies(slot, lo, hi):
+        index = RELAYED.index(slot)
+        return [
+            (
+                condition,
+                pltpu.make_async_remote_copy(
+                    src_ref=relay.at[index], dst_ref=target,
+                    send_sem=relay_send_sem.at[index], recv_sem=halo_recv_sem.at[side, slot],
+                    device_id={"gx": neighbour}, device_id_type=MESH,
+                ),
+                pltpu.make_async_remote_copy(
+                    src_ref=relay.at[index], dst_ref=relay.at[index],
+                    send_sem=relay_send_sem.at[index], recv_sem=relay_recv_sem.at[index],
+                    device_id={"gx": neighbour}, device_id_type=MESH,
+                ),
+            )
+            for side, condition, target, neighbour in (
+                (0, relays_up, lo, left),
+                (1, relays_down, hi, right),
+            )
+        ]
+
+    def relay_start(copies):
+        for condition, forward, arrival in copies:
+
+            @pl.when(condition)
+            def _(forward=forward, arrival=arrival):
+                arrival.wait_recv()
+                forward.start()
 
     def edge_store(source, slot):
         edges[slot, 0, 0] = source[CX - 3] + OUTERMOST * source[CX - 4]
@@ -283,14 +345,24 @@
     for f in range(5):
         edge_store(sources[f], f)
 
-    pl.semaphore_wait(barrier, GY + 1)
+    at_end = jnp.logical_or(first_in_run, last_in_run)
+
+    @pl.when(at_end)
+    def _():
+        pl.semaphore_wait(barrier, GY + 2)
+
+    @pl.when(jnp.logical_not(at_end))
+    def _():
+        pl.semaphore_wait(barrier, GY + 1)
+
+    halos = [halo_pair(halo_lo.at[f], halo_hi.at[f], f) for f in range(5)]
+    for f in (2, 0):
+        halo_start(halos[f], f)
     a2a_start(0, speed_send, speed_recv)
     a2a_start(1, state_send, state_recv)
 
-    halos = [halo_pair(halo_lo.at[f], halo_hi.at[f], f) for f in range(5)]
-    for f in (2, 0, 1, 3, 4):
-        for copy in halos[f]:
-            copy.start()
+    for f in (1, 3, 4):
+        halo_start(halos[f], f)
 
     loads[3].wait()
 
@@ -335,6 +407,9 @@
 
     lax.fori_loop(0, CX, extras, 0)
     a2a_start(2, cross_send, cross_recv)
+    relays = [relay_copies(f, halo_lo.at[f], halo_hi.at[f]) for f in (1, 3, 4)]
+    for copies in relays:
+        relay_start(copies)
 
     def build(fields):
         def body(s, carry):
@@ -485,8 +560,7 @@
     flux_halos = [halo_pair(flux_lo.at[f], flux_hi.at[f], 5 + f) for f in range(4)]
     for f in range(4):
         edge_store(flux_x.at[f], 5 + f)
-        for copy in flux_halos[f]:
-            copy.start()
+        halo_start(flux_halos[f], 5 + f)
 
     a2a_wait_recv(4, slope2_send, slope2_recv)
 
@@ -511,6 +585,10 @@
     for f in range(1, 5):
         out_ref[f] = pitch_derivative(f)
 
+    relays += [relay_copies(5 + f, flux_lo.at[f], flux_hi.at[f]) for f in (2, 3)]
+    for copies in relays[3:]:
+        relay_start(copies)
+
     def accumulate(f, own, lo, hi):
         def emit(i, rows, value):
             out_ref[f, i, rows] += value
@@ -540,6 +618,13 @@
     a2a_wait_send(5, div_send, div_recv)
     for copy in siblings:
         copy.wait_send()
+    for copies in relays:
+        for condition, forward, _ in copies:
+
+            @pl.when(condition)
+            def _(forward=forward):
+                forward.wait_send()
+
     for copies in halos + flux_halos:
         for copy in copies:
             copy.wait_send()
@@ -592,6 +677,9 @@
             pltpu.SemaphoreType.DMA((6, GY - 1)),
             pltpu.SemaphoreType.DMA((2, 9)),
             pltpu.SemaphoreType.DMA((2, 9)),
+            pltpu.VMEM((len(RELAYED), EDGE, ZB, NY), f32),
+            pltpu.SemaphoreType.DMA((len(RELAYED),)),
+            pltpu.SemaphoreType.DMA((len(RELAYED),)),
         ],
         compiler_params=pltpu.CompilerParams(
             collective_id=0, has_side_effects=True, vmem_limit_bytes=24 * 1024 * 1024

time: 54.2 us -> 49.9 us (0.921)
  the two profiles are of different devices: /device:TPU:1 before, /device:TPU:8 now
where the time goes in v4:
time: 49.9 us; the launch traced here: 49.7 us
  Pallas kernels  47.8 us (96%)
  other arithmetic  1.25 us (3%)
  between operations  0.64 us (1%)
    pallas_call x1, Pallas kernels, per_device(): pl.pallas_call(kernel, out_shape=[jax.ShapeDtypeStruct((5,) + field, f32)...  47.8 us
    add x1, other arithmetic, per_device(): return (tendency, conserved + section_step * tendency)  1.25 us

profile of v4, /device:TPU:8, one launch (start us, length us, event | category | flops | bytes accessed | tf_op | source)
XLA Modules:
  0.0 49.7 jit_solution(2419196776526393864)
XLA Ops:
  0.6 47.8 %shard_map.86 = (f32[5,8,32,128]{3,2,1,0:T(8,128)S(1)}, f32[5,8,32,128]{3,2,1,0:T(8,128)S(1)}) custom-call(f32[8,32,128]{2,1,0:T(8,128)} %rho_hbm.1, f32[3,8,32,128]{3,2,1,0:T(8,128)} %mom_hbm.1, f32[8,32,128]{2,1,0:T(8,128)} %en_hbm.1, bf16[256,512]{1,0:T(8,128)(2,1)} %constant.10.clone.dh_hbm, bf16[256,512]{1,0:T(8,128)(2,1)} %constant.11.clone.dl_hbm, ...), custom_call_target="tpu_custom_call" | custom-call | tf_op jit(solution)/shard_map/pallas_call | solution.py:639
  48.5 1.3 %multiply_add_fusion = (f32[5,8,32,128]{3,2,1,0:T(8,128)}, f32[5,8,32,128]{3,2,1,0:T(8,128)}) fusion(f32[5,8,32,128]{3,2,1,0:T(8,128)S(1)} %get-tuple-element.5, f32[5,8,32,128]{3,2,1,0:T(8,128)S(1)} %get-tuple-element.4), kind=kLoop, calls=%fused_computation | loop fusion | flops 491520 | bytes 2621440 | tf_op jit(solution)/shard_map/add | solution.py:689

commit v5 on v4

--- a/solution.py
+++ b/solution.py
@@ -139,7 +139,7 @@
 
 
 RUN = 16
-RELAYED = (1, 3, 4, 7, 8)
+RELAYED = (1, 3, 4)
 STEPS = [
     (dx, dy, dc)
     for dc in range(2)
@@ -155,6 +155,7 @@
     grad_x, grad_y, flux_x, keep, pitch_in, span_x, rhs_h, rhs_l, dz_t, span_visc,
     sib_value, sib_send_buf, span_in, span_dy, dz_v2, sib_send_sem, sib_recv_sem,
     load_sem, a2a_send_sem, a2a_recv_sem, halo_send_sem, halo_recv_sem, relay, relay_send_sem, relay_recv_sem,
+    word_sem,
 ):
     gx = lax.axis_index("gx")
     me = lax.axis_index("gy")
@@ -180,10 +181,27 @@
 
     barrier = pltpu.get_barrier_semaphore()
     sibling = partners[-1]
-    for partner in partners:
-        pl.semaphore_signal(barrier, inc=1, device_id={"gy": partner}, device_id_type=MESH)
+    for (_, _, dc), partner in zip(STEPS, partners):
+
+        @pl.when(lax.rem(core + dc, 2) == 0)
+        def _(partner=partner):
+            pl.semaphore_signal(barrier, inc=1, device_id={"gy": partner}, device_id_type=MESH)
+
+    gatherer = me - core + 1
+
+    def greet(neighbour):
+        pl.semaphore_signal(
+            barrier, inc=1, device_id={"gx": neighbour, "gy": gatherer}, device_id_type=MESH
+        )
+
     for neighbour in (left, right):
-        pl.semaphore_signal(barrier, inc=1, device_id={"gx": neighbour}, device_id_type=MESH)
+        greet(neighbour)
+
+    def pass_word():
+        pl.semaphore_signal(word_sem, inc=1, device_id={"gy": sibling}, device_id_type=MESH)
+
+    def hear_word():
+        pl.semaphore_wait(word_sem, 1)
 
     run = lax.rem(gx, RUN)
     first_in_run, last_in_run = run == 0, run == RUN - 1
@@ -193,7 +211,7 @@
 
         @pl.when(condition)
         def _(source=source):
-            pl.semaphore_signal(barrier, inc=1, device_id={"gx": source}, device_id_type=MESH)
+            greet(source)
 
     low_lanes = lax.broadcasted_iota(jnp.int32, (HZ, NY), 1) < NY // 2
 
@@ -346,20 +364,45 @@
         edge_store(sources[f], f)
 
     at_end = jnp.logical_or(first_in_run, last_in_run)
-
-    @pl.when(at_end)
+    halos = [halo_pair(halo_lo.at[f], halo_hi.at[f], f) for f in range(5)]
+
+    @pl.when(core == 0)
     def _():
-        pl.semaphore_wait(barrier, GY + 2)
-
-    @pl.when(jnp.logical_not(at_end))
+        pl.semaphore_wait(barrier, GY - 1)
+        pass_word()
+
+    @pl.when(core == 1)
     def _():
-        pl.semaphore_wait(barrier, GY + 1)
-
-    halos = [halo_pair(halo_lo.at[f], halo_hi.at[f], f) for f in range(5)]
-    for f in (2, 0):
-        halo_start(halos[f], f)
+        hear_word()
+
+    def meet():
+        @pl.when(jnp.logical_and(core == 1, at_end))
+        def _():
+            pl.semaphore_wait(barrier, 6)
+            pass_word()
+
+        @pl.when(jnp.logical_and(core == 1, jnp.logical_not(at_end)))
+        def _():
+            pl.semaphore_wait(barrier, 4)
+            pass_word()
+
+        @pl.when(core == 0)
+        def _():
+            hear_word()
+
+        for f in (2, 0):
+            halo_start(halos[f], f)
+
+    @pl.when(jnp.logical_not(first_in_run))
+    def _():
+        meet()
+
     a2a_start(0, speed_send, speed_recv)
     a2a_start(1, state_send, state_recv)
+
+    @pl.when(first_in_run)
+    def _():
+        meet()
 
     for f in (1, 3, 4):
         halo_start(halos[f], f)
@@ -397,16 +440,20 @@
 
         stream_derivative(sources[f], halo_lo.at[f], halo_hi.at[f], emit)
 
-    prim_x(2)
-    prim_x(0)
-
-    def extras(x, carry):
-        pack(cross_send, 0, x, grad_x[2, x])
-        pack(cross_send, 1, x, grad_x[0, x])
-        return carry
-
-    lax.fori_loop(0, CX, extras, 0)
-    a2a_start(2, cross_send, cross_recv)
+    def cross():
+        prim_x(2)
+        prim_x(0)
+
+        def extras(x, carry):
+            pack(cross_send, 0, x, grad_x[2, x])
+            pack(cross_send, 1, x, grad_x[0, x])
+            return carry
+
+        lax.fori_loop(0, CX, extras, 0)
+        a2a_start(2, cross_send, cross_recv)
+
+    cross()
+
     relays = [relay_copies(f, halo_lo.at[f], halo_hi.at[f]) for f in (1, 3, 4)]
     for copies in relays:
         relay_start(copies)
@@ -584,10 +631,6 @@
     out_ref[0] += pitch_derivative(0)
     for f in range(1, 5):
         out_ref[f] = pitch_derivative(f)
-
-    relays += [relay_copies(5 + f, flux_lo.at[f], flux_hi.at[f]) for f in (2, 3)]
-    for copies in relays[3:]:
-        relay_start(copies)
 
     def accumulate(f, own, lo, hi):
         def emit(i, rows, value):
@@ -680,6 +723,7 @@
             pltpu.VMEM((len(RELAYED), EDGE, ZB, NY), f32),
             pltpu.SemaphoreType.DMA((len(RELAYED),)),
             pltpu.SemaphoreType.DMA((len(RELAYED),)),
+            pltpu.SemaphoreType.REGULAR,
         ],
         compiler_params=pltpu.CompilerParams(
             collective_id=0, has_side_effects=True, vmem_limit_bytes=24 * 1024 * 1024

time: 49.9 us -> 46.8 us (0.938)
  the two profiles are of different devices: /device:TPU:8 before, /device:TPU:1 now
where the time goes in v5:
time: 46.8 us; the launch traced here: 46.6 us
  Pallas kernels  44.8 us (96%)
  other arithmetic  1.25 us (3%)
  between operations  0.64 us (1%)
    pallas_call x1, Pallas kernels, per_device(): pl.pallas_call(kernel, out_shape=[jax.ShapeDtypeStruct((5,) + field, f32)...  44.8 us
    add x1, other arithmetic, per_device(): return (tendency, conserved + section_step * tendency)  1.25 us

profile of v5, /device:TPU:1, one launch (start us, length us, event | category | flops | bytes accessed | tf_op | source)
XLA Modules:
  0.0 46.6 jit_solution(12689450037122712879)
XLA Ops:
  0.6 44.8 %shard_map.86 = (f32[5,8,32,128]{3,2,1,0:T(8,128)S(1)}, f32[5,8,32,128]{3,2,1,0:T(8,128)S(1)}) custom-call(f32[8,32,128]{2,1,0:T(8,128)} %rho_hbm.1, f32[3,8,32,128]{3,2,1,0:T(8,128)} %mom_hbm.1, f32[8,32,128]{2,1,0:T(8,128)} %en_hbm.1, bf16[256,512]{1,0:T(8,128)(2,1)} %constant.10.clone.dh_hbm, bf16[256,512]{1,0:T(8,128)(2,1)} %constant.11.clone.dl_hbm, ...), custom_call_target="tpu_custom_call" | custom-call | tf_op jit(solution)/shard_map/pallas_call | solution.py:682
  45.4 1.3 %multiply_add_fusion = (f32[5,8,32,128]{3,2,1,0:T(8,128)}, f32[5,8,32,128]{3,2,1,0:T(8,128)}) fusion(f32[5,8,32,128]{3,2,1,0:T(8,128)S(1)} %get-tuple-element.5, f32[5,8,32,128]{3,2,1,0:T(8,128)S(1)} %get-tuple-element.4), kind=kLoop, calls=%fused_computation | loop fusion | flops 491520 | bytes 2621440 | tf_op jit(solution)/shard_map/add | solution.py:733

commit v6 on v5

--- a/solution.py
+++ b/solution.py
@@ -390,7 +390,7 @@
         def _():
             hear_word()
 
-        for f in (2, 0):
+        for f in (2, 0, 1, 3, 4):
             halo_start(halos[f], f)
 
     @pl.when(jnp.logical_not(first_in_run))
@@ -404,8 +404,6 @@
     def _():
         meet()
 
-    for f in (1, 3, 4):
-        halo_start(halos[f], f)
 
     loads[3].wait()
 
@@ -550,6 +548,41 @@
 
     prim_x(1)
     prim_x(3)
+
+    flux_halos = [halo_pair(flux_lo.at[f], flux_hi.at[f], 5 + f) for f in range(4)]
+    def stream_part():
+        a2a_wait_recv(3, slope_send, slope_recv)
+
+        def stream_flux(x, carry):
+            dz1, dz3 = unpack(slope_recv, 0, x), unpack(slope_recv, 1, x)
+            density, m1, m2, m3, energy = [con[f, x] for f in range(5)]
+            v1, v2, v3, temperature = [prim[f, x] for f in range(4)]
+            pressure = temperature * density
+            dx1, dx2, dx3, dxt = [grad_x[f, x] for f in range(4)]
+            visc = keep[0, x]
+            bulk = (2.0 / 3.0) * (dx1 + grad_y[1, x] + dz3)
+            s11 = visc * (2.0 * dx1 - bulk)
+            s12 = visc * (dx2 + grad_y[0, x])
+            s13 = visc * (dx3 + dz1)
+            flux_x[0, x] = m1 * v1 + pressure - s11
+            flux_x[1, x] = m2 * v1 - s12
+            flux_x[2, x] = m3 * v1 - s13
+            work = s11 * v1 + s12 * v2 + s13 * v3
+            flux_x[3, x] = (energy + pressure) * v1 - work - (visc * conduction) * dxt
+            keep[1, x] = bulk
+            keep[2, x] = s12
+            return carry
+
+        lax.fori_loop(0, CX, stream_flux, 0)
+        for f in range(4):
+            edge_store(flux_x.at[f], 5 + f)
+            halo_start(flux_halos[f], 5 + f)
+
+    flux_early = last_in_run
+
+    @pl.when(flux_early)
+    def _():
+        stream_part()
 
     a2a_wait_recv(2, cross_send, cross_recv)
 
@@ -581,33 +614,9 @@
             div_send[:, pair + f] = value - span_dy[pair + f] if pair else value
     a2a_start(5, div_send, div_recv)
 
-    a2a_wait_recv(3, slope_send, slope_recv)
-
-    def stream_flux(x, carry):
-        dz1, dz3 = unpack(slope_recv, 0, x), unpack(slope_recv, 1, x)
-        density, m1, m2, m3, energy = [con[f, x] for f in range(5)]
-        v1, v2, v3, temperature = [prim[f, x] for f in range(4)]
-        pressure = temperature * density
-        dx1, dx2, dx3, dxt = [grad_x[f, x] for f in range(4)]
-        visc = keep[0, x]
-        bulk = (2.0 / 3.0) * (dx1 + grad_y[1, x] + dz3)
-        s11 = visc * (2.0 * dx1 - bulk)
-        s12 = visc * (dx2 + grad_y[0, x])
-        s13 = visc * (dx3 + dz1)
-        flux_x[0, x] = m1 * v1 + pressure - s11
-        flux_x[1, x] = m2 * v1 - s12
-        flux_x[2, x] = m3 * v1 - s13
-        work = s11 * v1 + s12 * v2 + s13 * v3
-        flux_x[3, x] = (energy + pressure) * v1 - work - (visc * conduction) * dxt
-        keep[1, x] = bulk
-        keep[2, x] = s12
-        return carry
-
-    lax.fori_loop(0, CX, stream_flux, 0)
-    flux_halos = [halo_pair(flux_lo.at[f], flux_hi.at[f], 5 + f) for f in range(4)]
-    for f in range(4):
-        edge_store(flux_x.at[f], 5 + f)
-        halo_start(flux_halos[f], 5 + f)
+    @pl.when(jnp.logical_not(flux_early))
+    def _():
+        stream_part()
 
     a2a_wait_recv(4, slope2_send, slope2_recv)
 

time: 46.8 us -> 46 us (0.983)
  Pallas kernels: 44.8 us -> 43.9 us
    pallas_call x1, Pallas kernels: 44.8 us -> 43.9 us  [per_device(): pl.pallas_call(kernel, out_shape=[jax.ShapeDtypeStruct((5,) + field, f32)...]
where the time goes in v6:
time: 46 us; the launch traced here: 45.8 us
  Pallas kernels  43.9 us (95%)
  other arithmetic  1.25 us (3%)
  between operations  0.64 us (1%)
    pallas_call x1, Pallas kernels, per_device(): pl.pallas_call(kernel, out_shape=[jax.ShapeDtypeStruct((5,) + field, f32)...  43.9 us
    add x1, other arithmetic, per_device(): return (tendency, conserved + section_step * tendency)  1.25 us

profile of v6, /device:TPU:1, one launch (start us, length us, event | category | flops | bytes accessed | tf_op | source)
XLA Modules:
  0.0 45.8 jit_solution(2741399397636810037)
XLA Ops:
  0.6 43.9 %shard_map.86 = (f32[5,8,32,128]{3,2,1,0:T(8,128)S(1)}, f32[5,8,32,128]{3,2,1,0:T(8,128)S(1)}) custom-call(f32[8,32,128]{2,1,0:T(8,128)} %rho_hbm.1, f32[3,8,32,128]{3,2,1,0:T(8,128)} %mom_hbm.1, f32[8,32,128]{2,1,0:T(8,128)} %en_hbm.1, bf16[256,512]{1,0:T(8,128)(2,1)} %constant.10.clone.dh_hbm, bf16[256,512]{1,0:T(8,128)(2,1)} %constant.11.clone.dl_hbm, ...), custom_call_target="tpu_custom_call" | custom-call | tf_op jit(solution)/shard_map/pallas_call | solution.py:691
  44.6 1.3 %multiply_add_fusion = (f32[5,8,32,128]{3,2,1,0:T(8,128)}, f32[5,8,32,128]{3,2,1,0:T(8,128)}) fusion(f32[5,8,32,128]{3,2,1,0:T(8,128)S(1)} %get-tuple-element.5, f32[5,8,32,128]{3,2,1,0:T(8,128)S(1)} %get-tuple-element.4), kind=kLoop, calls=%fused_computation | loop fusion | flops 491520 | bytes 2621440 | tf_op jit(solution)/shard_map/add | solution.py:742

commit v7 on v6

--- a/solution.py
+++ b/solution.py
@@ -649,18 +649,27 @@
 
     halo_wait(halos[4])
     accumulate(0, con.at[1], halo_lo.at[4], halo_hi.at[4])
+    def add_span():
+        a2a_wait_recv(5, div_send, div_recv)
+
+        def last(x, carry):
+            for f in range(4):
+                out_ref[1 + f, x] += unpack(div_recv, f, x)
+            return carry
+
+        lax.fori_loop(0, CX, last, 0)
+
+    @pl.when(first_in_run)
+    def _():
+        add_span()
+
     for f in range(4):
         halo_wait(flux_halos[f])
         accumulate(1 + f, flux_x.at[f], flux_lo.at[f], flux_hi.at[f])
 
-    a2a_wait_recv(5, div_send, div_recv)
-
-    def last(x, carry):
-        for f in range(4):
-            out_ref[1 + f, x] += unpack(div_recv, f, x)
-        return carry
-
-    lax.fori_loop(0, CX, last, 0)
+    @pl.when(jnp.logical_not(first_in_run))
+    def _():
+        add_span()
 
     a2a_wait_send(0, speed_send, speed_recv)
     a2a_wait_send(1, state_send, state_recv)

time: 46 us -> 45.3 us (0.985)
  Pallas kernels: 43.9 us -> 43.2 us
    pallas_call x1, Pallas kernels: 43.9 us -> 43.2 us  [per_device(): pl.pallas_call(kernel, out_shape=[jax.ShapeDtypeStruct((5,) + field, f32)...]
where the time goes in v7:
time: 45.3 us; the launch traced here: 45.1 us
  Pallas kernels  43.2 us (95%)
  other arithmetic  1.25 us (3%)
  between operations  0.64 us (1%)
    pallas_call x1, Pallas kernels, per_device(): pl.pallas_call(kernel, out_shape=[jax.ShapeDtypeStruct((5,) + field, f32)...  43.2 us
    add x1, other arithmetic, per_device(): return (tendency, conserved + section_step * tendency)  1.25 us

profile of v7, /device:TPU:1, one launch (start us, length us, event | category | flops | bytes accessed | tf_op | source)
XLA Modules:
  0.0 45.1 jit_solution(10954591999415223556)
XLA Ops:
  0.6 43.2 %shard_map.86 = (f32[5,8,32,128]{3,2,1,0:T(8,128)S(1)}, f32[5,8,32,128]{3,2,1,0:T(8,128)S(1)}) custom-call(f32[8,32,128]{2,1,0:T(8,128)} %rho_hbm.1, f32[3,8,32,128]{3,2,1,0:T(8,128)} %mom_hbm.1, f32[8,32,128]{2,1,0:T(8,128)} %en_hbm.1, bf16[256,512]{1,0:T(8,128)(2,1)} %constant.10.clone.dh_hbm, bf16[256,512]{1,0:T(8,128)(2,1)} %constant.11.clone.dl_hbm, ...), custom_call_target="tpu_custom_call" | custom-call | tf_op jit(solution)/shard_map/pallas_call | solution.py:700
  43.8 1.3 %multiply_add_fusion = (f32[5,8,32,128]{3,2,1,0:T(8,128)}, f32[5,8,32,128]{3,2,1,0:T(8,128)}) fusion(f32[5,8,32,128]{3,2,1,0:T(8,128)S(1)} %get-tuple-element.5, f32[5,8,32,128]{3,2,1,0:T(8,128)S(1)} %get-tuple-element.4), kind=kLoop, calls=%fused_computation | loop fusion | flops 491520 | bytes 2621440 | tf_op jit(solution)/shard_map/add | solution.py:751
